TPU v7x, 32 devices: a whole 2x2x4 slice. The times are simulated.
32 devices in a mesh: ctx: 8 (over z, core), fsdp: 4 (over y, x).
Axes of the slice: x: 2, y: 2, z: 4, core: 2. Of those that a mesh axis runs over, the one named last changes fastest.
Arguments:
- block_input: bfloat16 [2, 4, 2048, 767], P(None, 'fsdp', 'ctx'), may hold values from -6 to 6
- cotangent: bfloat16 [2, 4, 2048, 767], P(None, 'fsdp', 'ctx'), may hold values from -6 to 6
- segment_ids: int32 [2, 4, 2048], P(None, 'fsdp'), may hold values from 0 to 7, never falling along the last dimension, each value on 1 to 512 neighbouring positions
- block_order: int32 [16], replicated, may hold values from 0 to 15, as said below
- gain_attn: bfloat16 [2, 768], P(None, 'fsdp'), may hold values from 0.5 to 1.5
- w_qkv: bfloat16 [2, 768, 2304], P(None, 'fsdp'), may hold values from -0.21875 to 0.21875
- bias_q: bfloat16 [2, 768], P(None, 'fsdp'), may hold values from -3 to 3
- bias_v: bfloat16 [2, 768], P(None, 'fsdp'), may hold values from -3 to 3
- w_out: bfloat16 [2, 768, 768], P(None, 'fsdp'), may hold values from -1.75 to 1.75
- bias_out: bfloat16 [2, 768], P(None, 'fsdp'), may hold values from -3 to 3
- gain_mlp: bfloat16 [2, 768], P(None, 'fsdp'), may hold values from 0.5 to 1.5
- w_up: bfloat16 [2, 768, 3072], P(None, 'fsdp'), may hold values from -0.21875 to 0.21875
- bias_up: bfloat16 [2, 3072], P(None, 'fsdp'), may hold values from -3 to 3
- w_down: bfloat16 [2, 3072, 768], P(None, 'fsdp'), may hold values from -0.109375 to 0.109375
- bias_down: bfloat16 [2, 768], P(None, 'fsdp'), may hold values from -3 to 3
Outputs:
- block_output: bfloat16 [2, 4, 2048, 767], P(None, 'fsdp', 'ctx')
- grad_input: float32 [2, 4, 2048, 767], P(None, 'fsdp', 'ctx')
- grad_gain_attn: float32 [2, 768], P(None, 'fsdp')
- grad_w_qkv: float32 [2, 768, 2304], P(None, 'fsdp')
- grad_bias_q: float32 [2, 768], P(None, 'fsdp')
- grad_bias_v: float32 [2, 768], P(None, 'fsdp')
- grad_w_out: float32 [2, 768, 768], P(None, 'fsdp')
- grad_bias_out: float32 [2, 768], P(None, 'fsdp')
- grad_gain_mlp: float32 [2, 768], P(None, 'fsdp')
- grad_w_up: float32 [2, 768, 3072], P(None, 'fsdp')
- grad_bias_up: float32 [2, 3072], P(None, 'fsdp')
- grad_w_down: float32 [2, 3072, 768], P(None, 'fsdp')
- grad_bias_down: float32 [2, 768], P(None, 'fsdp')
Inputs may be any that keep to these rules, and one draw needn't show every extreme that they name: `block_order`: entries 2c and 2c + 1 hold blocks p and 15 - p of the sequence for some p, the lower first; each block appears once. `segment_ids`: along each sequence the document numbers never fall and each of the 8 documents holds 1 to 512 tokens, one exactly 512.
All inputs are finite; a program needn't handle non-finite values.
Results may differ from a plain program's by a relative error of at most 0.022.
Values may be sent and summed in bfloat16 or wider, within the bound.
A program may use at most 384 MiB of HBM per device.

v0:
```python
from functools import partial

import jax
import jax.numpy as jnp
from jax import lax
from jax.experimental import pallas as pl
from jax.experimental.pallas import tpu as pltpu
from jax.sharding import PartitionSpec as P

HD = 64
EPS = 1e-06
NEG = -1e30
BF = jnp.bfloat16
F32 = jnp.float32
QT = 256


def tile_spans(rows, halo, tile):
    return [(i, (i, halo), (0, i + tile)) for i in range(0, rows, tile)]


def tile_masks(seg_q, seg_own, seg_halo, row0, halo_span, own_span, tile):
    h0, h1 = halo_span
    o0, o1 = own_span
    seg_rows = seg_q[row0 : row0 + tile, :]
    row = row0 + lax.broadcasted_iota(jnp.int32, (tile, o1 - o0), 0)
    col = o0 + lax.broadcasted_iota(jnp.int32, (tile, o1 - o0), 1)
    own = (seg_rows == seg_own[:, o0:o1]) & (col <= row)
    past = seg_rows == seg_halo[:, h0:h1] if h1 > h0 else None
    return past, own


def dot_t(a, b):
    return lax.dot_general(a, b, (((1,), (1,)), ((), ())), preferred_element_type=F32)


def dot_n(a, b):
    return lax.dot_general(a, b, (((1,), (0,)), ((), ())), preferred_element_type=F32)


def dot_l(a, b):
    return lax.dot_general(a, b, (((0,), (0,)), ((), ())), preferred_element_type=F32)


def attend_kernel(q_ref, k_ref, v_ref, kh_ref, vh_ref, sq_ref, so_ref, sh_ref, o_ref, lse_ref):
    rows, halo = q_ref.shape[0], kh_ref.shape[0]
    scale = HD ** (-0.5)
    seg_q, seg_own, seg_halo = sq_ref[...], so_ref[...], sh_ref[...]
    for row0, (h0, h1), (o0, o1) in tile_spans(rows, halo, QT):
        past, own = tile_masks(seg_q, seg_own, seg_halo, row0, (h0, h1), (o0, o1), QT)
        for j in range(2):
            cols = slice(j * HD, (j + 1) * HD)
            q = q_ref[row0 : row0 + QT, cols]
            s_own = jnp.where(own, dot_t(q, k_ref[o0:o1, cols]) * scale, NEG)
            top = jnp.max(s_own, axis=-1, keepdims=True)
            if past is not None:
                s_past = jnp.where(past, dot_t(q, kh_ref[h0:h1, cols]) * scale, NEG)
                top = jnp.maximum(top, jnp.max(s_past, axis=-1, keepdims=True))
            e_own = jnp.exp(s_own - top)
            total = jnp.sum(e_own, axis=-1, keepdims=True)
            out = dot_n(e_own.astype(BF), v_ref[o0:o1, cols])
            if past is not None:
                e_past = jnp.exp(s_past - top)
                total = total + jnp.sum(e_past, axis=-1, keepdims=True)
                out = out + dot_n(e_past.astype(BF), vh_ref[h0:h1, cols])
            o_ref[row0 : row0 + QT, cols] = (out / total).astype(BF)
            lse_ref[row0 : row0 + QT, cols] = jnp.broadcast_to(top + jnp.log(total), (QT, HD))


def attend_forward(qkv, kv_halo, segs):
    rows, width = qkv.shape[0], qkv.shape[1] // 3
    halo = kv_halo.shape[0]
    pairs = width // (2 * HD)
    seg_q, seg_own, seg_halo = segs
    col = lambda off: (lambda h: (0, off + h))
    fixed = lambda h: (0, 0)
    return pl.pallas_call(
        attend_kernel,
        name="attend_forward",
        grid=(pairs,),
        in_specs=[
            pl.BlockSpec((rows, 2 * HD), col(0)),
            pl.BlockSpec((rows, 2 * HD), col(pairs)),
            pl.BlockSpec((rows, 2 * HD), col(2 * pairs)),
            pl.BlockSpec((halo, 2 * HD), col(0)),
            pl.BlockSpec((halo, 2 * HD), col(pairs)),
            pl.BlockSpec((rows, 1), fixed),
            pl.BlockSpec((1, rows), fixed),
            pl.BlockSpec((1, halo), fixed),
        ],
        out_specs=[
            pl.BlockSpec((rows, 2 * HD), col(0)),
            pl.BlockSpec((rows, 2 * HD), col(0)),
        ],
        out_shape=[
            jax.ShapeDtypeStruct((rows, width), BF),
            jax.ShapeDtypeStruct((rows, width), F32),
        ],
        cost_estimate=pl.CostEstimate(
            flops=4 * rows * (rows + halo) * width,
            transcendentals=rows * (rows + halo) * pairs * 2,
            bytes_accessed=12 * rows * width,
        ),
    )(qkv, qkv, qkv, kv_halo, kv_halo, seg_q, seg_own, seg_halo)


def attend_back_kernel(
    q_ref, k_ref, v_ref, kh_ref, vh_ref, do_ref, lse_ref, sq_ref, so_ref, sh_ref,
    dq_ref, dk_ref, dv_ref, dkh_ref, dvh_ref,
    ak_ref, av_ref, akh_ref, avh_ref,
):
    rows, halo = q_ref.shape[0], kh_ref.shape[0]
    scale = HD ** (-0.5)
    seg_q, seg_own, seg_halo = sq_ref[...], so_ref[...], sh_ref[...]
    for ref in (ak_ref, av_ref, akh_ref, avh_ref):
        ref[...] = jnp.zeros_like(ref)
    for row0, (h0, h1), (o0, o1) in tile_spans(rows, halo, QT):
        past, own = tile_masks(seg_q, seg_own, seg_halo, row0, (h0, h1), (o0, o1), QT)
        tile = slice(row0, row0 + QT)
        for j in range(2):
            cols = slice(j * HD, (j + 1) * HD)
            q = q_ref[tile, cols]
            do = do_ref[tile, cols]
            lse = lse_ref[tile, j * HD : j * HD + 1]
            parts = [(own, k_ref, v_ref, ak_ref, av_ref, slice(o0, o1))]
            if past is not None:
                parts.append((past, kh_ref, vh_ref, akh_ref, avh_ref, slice(h0, h1)))
            work = []
            inner = jnp.zeros((QT, 1), F32)
            for mask, kr, vr, akr, avr, span in parts:
                k, v = kr[span, cols], vr[span, cols]
                p = jnp.exp(jnp.where(mask, dot_t(q, k) * scale, NEG) - lse)
                dp = dot_t(do, v)
                inner = inner + jnp.sum(p * dp, axis=-1, keepdims=True)
                work.append((p, dp, k, akr, avr, span))
            dq = jnp.zeros((QT, HD), F32)
            for p, dp, k, akr, avr, span in work:
                ds = (p * (dp - inner) * scale).astype(BF)
                dq = dq + dot_n(ds, k)
                akr[span, cols] += dot_l(ds, q)
                avr[span, cols] += dot_l(p.astype(BF), do)
            dq_ref[tile, cols] = dq.astype(BF)
    dk_ref[...] = ak_ref[...]
    dv_ref[...] = av_ref[...]
    dkh_ref[...] = akh_ref[...].astype(BF)
    dvh_ref[...] = avh_ref[...].astype(BF)


def attend_backward(qkv, kv_halo, segs, lse, d_mixed):
    rows, width = qkv.shape[0], qkv.shape[1] // 3
    halo = kv_halo.shape[0]
    pairs = width // (2 * HD)
    seg_q, seg_own, seg_halo = segs
    col = lambda off: (lambda h: (0, off + h))
    fixed = lambda h: (0, 0)
    own = lambda off: pl.BlockSpec((rows, 2 * HD), col(off))
    past = lambda off: pl.BlockSpec((halo, 2 * HD), col(off))
    return pl.pallas_call(
        attend_back_kernel,
        name="attend_backward",
        grid=(pairs,),
        in_specs=[
            own(0), own(pairs), own(2 * pairs), past(0), past(pairs), own(0), own(0),
            pl.BlockSpec((rows, 1), fixed),
            pl.BlockSpec((1, rows), fixed),
            pl.BlockSpec((1, halo), fixed),
        ],
        out_specs=[own(0), own(0), own(0), past(0), past(0)],
        out_shape=[
            jax.ShapeDtypeStruct((rows, width), BF),
            jax.ShapeDtypeStruct((rows, width), F32),
            jax.ShapeDtypeStruct((rows, width), F32),
            jax.ShapeDtypeStruct((halo, width), BF),
            jax.ShapeDtypeStruct((halo, width), BF),
        ],
        scratch_shapes=[
            pltpu.VMEM((rows, 2 * HD), F32),
            pltpu.VMEM((rows, 2 * HD), F32),
            pltpu.VMEM((halo, 2 * HD), F32),
            pltpu.VMEM((halo, 2 * HD), F32),
        ],
        cost_estimate=pl.CostEstimate(
            flops=10 * rows * (rows + halo) * width,
            transcendentals=rows * (rows + halo) * pairs * 2,
            bytes_accessed=30 * rows * width,
        ),
    )(qkv, qkv, qkv, kv_halo, kv_halo, d_mixed, lse, seg_q, seg_own, seg_halo)


def mm(a, w):
    return jnp.dot(a, w, preferred_element_type=F32)


def mm_t(a, w):
    return lax.dot_general(a, w, (((1,), (1,)), ((), ())), preferred_element_type=F32)


def mm_l(a, b):
    return lax.dot_general(a, b, (((0,), (0,)), ((), ())), preferred_element_type=F32)


def off_mean(y):
    return y - jnp.mean(y, axis=-1, keepdims=True)


def inverse_rms(u):
    return lax.rsqrt(jnp.mean(u * u, axis=-1, keepdims=True) + EPS)


def halo_of(x, halo_steps, runs, axis_size):
    parts = []
    for step in range(halo_steps, 0, -1):
        pairs = [(i, i + step) for i in range(axis_size - step) if i % runs + step < runs]
        parts.append(lax.ppermute(x, "ctx", pairs))
    return jnp.concatenate(parts, axis=0) if len(parts) > 1 else parts[0]


def halo_back(d, own, halo_steps, runs, axis_size):
    rows = own.shape[0]
    for n, step in enumerate(range(halo_steps, 0, -1)):
        pairs = [(i + step, i) for i in range(axis_size - step) if i % runs + step < runs]
        own = own + lax.ppermute(d[n * rows : (n + 1) * rows], "ctx", pairs).astype(F32)
    return own


def layer_forward(u, w, segs, shift):
    gain_attn, w_qkv, bias_q, bias_v, w_out, bias_out, gain_mlp, w_up, bias_up, w_down, bias_down = w
    width = w_out.shape[0]
    a1 = (u * inverse_rms(u) * gain_attn).astype(BF)
    bias = jnp.concatenate([bias_q, jnp.zeros_like(bias_q), bias_v])
    qkv = (mm(a1, w_qkv) + bias).astype(BF)
    kv_halo = halo_of(qkv[:, width:], *shift)
    mixed, lse = attend_forward(qkv, kv_halo, segs)
    u1 = u + off_mean(mm(mixed, w_out) + bias_out)
    a2 = (u1 * inverse_rms(u1) * gain_mlp).astype(BF)
    z = mm(a2, w_up) + bias_up
    act = jax.nn.gelu(z, approximate=True).astype(BF)
    u2 = u1 + off_mean(mm(act, w_down) + bias_down)
    return u2, (u, a1, qkv, kv_halo, mixed, lse, u1, a2, z, act)


def norm_backward(d_normed, u, gain):
    r = inverse_rms(u)
    n = u * r
    d_gain = jnp.sum(d_normed * n, axis=0)
    e = d_normed * gain
    return r * (e - n * jnp.mean(e * n, axis=-1, keepdims=True)), d_gain


def column_sums(x):
    return jnp.sum(x.astype(F32), axis=0)


def layer_backward(g, kept, w, segs, shift):
    gain_attn, w_qkv, bias_q, bias_v, w_out, bias_out, gain_mlp, w_up, bias_up, w_down, bias_down = w
    u, a1, qkv, kv_halo, mixed, lse, u1, a2, z, act = kept
    width = w_out.shape[0]
    dy2 = off_mean(g).astype(BF)
    dw_down = mm_l(act, dy2)
    d_act = mm_t(dy2, w_down)
    pull = jax.vjp(partial(jax.nn.gelu, approximate=True), z)[1]
    dz = pull(d_act)[0].astype(BF)
    dw_up = mm_l(a2, dz)
    du1, dgain_mlp = norm_backward(mm_t(dz, w_up), u1, gain_mlp)
    g = g + du1
    dy = off_mean(g).astype(BF)
    dw_out = mm_l(mixed, dy)
    d_mixed = mm_t(dy, w_out).astype(BF)
    dq, dk, dv, dkh, dvh = attend_backward(qkv, kv_halo, segs, lse, d_mixed)
    dkv = halo_back(jnp.concatenate([dkh, dvh], axis=1), jnp.concatenate([dk, dv], axis=1), *shift)
    dqkv = jnp.concatenate([dq, dkv.astype(BF)], axis=1)
    dw_qkv = mm_l(a1, dqkv)
    sums = column_sums(dqkv)
    du, dgain_attn = norm_backward(mm_t(dqkv, w_qkv), u, gain_attn)
    grads = (
        dgain_attn, dw_qkv, sums[:width], sums[2 * width :], dw_out, column_sums(dy),
        dgain_mlp, dw_up, column_sums(dz), dw_down, column_sums(dy2),
    )
    return g + du, grads


def to_runs(x, block_order, size):
    batch, rows, width = x.shape
    block = rows // 2
    x = x.reshape(batch, 2, size, block // size, width).transpose(2, 0, 1, 3, 4)
    x = lax.all_to_all(x, "ctx", 0, 0, tiled=True)
    x = x.transpose(1, 0, 2, 3, 4).reshape(batch, 2 * size, block // size, width)
    x = jnp.take(x, jnp.argsort(block_order), axis=1)
    x = x.reshape(size, 2 * batch, block // size, width)
    x = lax.all_to_all(x, "ctx", 0, 0, tiled=True)
    return x.transpose(1, 0, 2, 3).reshape(batch * rows, width)


def from_runs(x, block_order, size, batch):
    rows, width = x.shape[0] // batch, x.shape[1]
    block = rows // 2
    x = x.reshape(2 * batch, size, block // size, width).transpose(1, 0, 2, 3)
    x = lax.all_to_all(x, "ctx", 0, 0, tiled=True)
    x = x.reshape(batch, 2 * size, block // size, width)
    x = jnp.take(x, block_order, axis=1)
    x = x.reshape(batch, size, 2, block // size, width).transpose(1, 0, 2, 3, 4)
    x = lax.all_to_all(x, "ctx", 0, 0, tiled=True)
    return x.transpose(1, 2, 0, 3, 4).reshape(batch, rows, width)


MESH = pl.DeviceIdType.MESH
COLOURS = ((0, 1, 2), (1, 2, 1))


def far(f, bit):
    return f + bit - 2 * bit * (f // bit % 2)


def remote(src, dst, send, recv, **device):
    return pltpu.make_async_remote_copy(src, dst, send, recv, device_id=device, device_id_type=MESH)


def greet(size, groups):
    barrier = pltpu.get_barrier_semaphore()
    f, c = lax.axis_index("fsdp"), lax.axis_index("ctx")
    for k in range(1, size):
        pl.semaphore_signal(barrier, inc=1, device_id={"ctx": (c + k) % size}, device_id_type=MESH)
    for k in range(1, groups):
        pl.semaphore_signal(barrier, inc=1, device_id={"fsdp": (f + k) % groups}, device_id_type=MESH)
    pl.semaphore_wait(barrier, size + groups - 2)


class Gather:
    flows = 6

    def __init__(self, source, shard, full, send, recv, pass_send, pass_recv, local, pending):
        self.source, self.shard, self.full, self.pending = source, shard, full, pending
        self.send, self.recv = send, recv
        self.pass_send, self.pass_recv, self.local = pass_send, pass_recv, local
        self.rows = shard.shape[0]
        self.f, c = lax.axis_index("fsdp"), lax.axis_index("ctx")
        self.core = c % 2
        self.sibling = c + 1 - 2 * self.core

    def piece(self, owner, q, core):
        size = self.rows // 4
        return self.full.at[pl.ds(owner * self.rows + core * 2 * size + q * size, size), :]

    def load(self):
        pltpu.make_async_copy(self.source, self.shard, self.local.at[0]).start()

    def first(self):
        size = self.rows // 4
        pltpu.make_async_copy(self.source, self.shard, self.local.at[0]).wait()
        for q, d1, d2 in COLOURS:
            own = self.shard.at[pl.ds(self.core * 2 * size + q * size, size), :]
            for k, d in enumerate((d1, d2)):
                flow = 3 * q + k
                copy = remote(
                    own, self.piece(self.f, q, self.core), self.send.at[flow], self.recv.at[flow],
                    fsdp=far(self.f, d),
                )
                copy.start()
                self.pending.append(copy.wait_send)
        copy = pltpu.make_async_copy(
            self.shard, self.full.at[pl.ds(self.f * self.rows, self.rows), :], self.local.at[1]
        )
        copy.start()
        self.pending.append(copy.wait)

    def land(self, q, k, owner):
        flow = 3 * q + k
        here = self.piece(owner, q, self.core)
        remote(here, here, self.send.at[flow], self.recv.at[flow], fsdp=owner).wait_recv()
        copy = remote(here, here, self.pass_send.at[flow], self.pass_recv.at[flow], ctx=self.sibling)
        copy.start()
        self.pending.append(copy.wait_send)
        there = self.piece(owner, q, 1 - self.core)
        self.pending.append(
            remote(there, there, self.pass_send.at[flow], self.pass_recv.at[flow], ctx=self.sibling).wait_recv
        )
        return here

    def second(self):
        for q, d1, d2 in COLOURS:
            here = self.land(q, 0, far(self.f, d1))
            copy = remote(
                here, here, self.send.at[3 * q + 2], self.recv.at[3 * q + 2], fsdp=far(self.f, d2)
            )
            copy.start()
            self.pending.append(copy.wait_send)
        for q, d1, d2 in COLOURS:
            self.land(q, 1, far(self.f, d2))

    def third(self):
        for q, d1, d2 in COLOURS:
            self.land(q, 2, far(far(self.f, 1), 2))


class Shuffle:
    def __init__(self, x, mid, turned, out, table, send, recv, local, pending, steps):
        self.x, self.mid, self.turned, self.out, self.table = x, mid, turned, out, table
        self.send, self.recv, self.local, self.pending = send, recv, local, pending
        self.size = x.shape[0]
        self.steps = steps

    def exchange(self, src, dst, phase):
        c = lax.axis_index("ctx")
        landed = []
        for k in range(1, self.size):
            to, come = (c + k) % self.size, (c + self.size - k) % self.size
            send, recv = self.send.at[phase, k - 1], self.recv.at[phase, k - 1]
            copy = remote(src.at[to], dst.at[c], send, recv, ctx=to)
            copy.start()
            self.pending.append(copy.wait_send)
            landed.append(remote(src.at[to], dst.at[come], send, recv, ctx=come).wait_recv)
        copy = pltpu.make_async_copy(src.at[c], dst.at[c], self.local.at[phase])
        copy.start()
        landed.append(copy.wait)
        return landed

    def first(self):
        self.landed = self.exchange(self.x, self.mid, 0)

    def second(self):
        for wait in self.landed:
            wait()
        for slot, part, entry in self.steps:
            self.turned[slot, part] = self.mid[self.table[0, entry], self.table[1, entry]]
        self.landed = self.exchange(self.turned, self.out, 1)

    def third(self):
        for wait in self.landed:
            wait()


def run_steps(size, batch):
    per = size // batch
    return [
        (b * per + r, k, b * 2 * size + 2 * batch * r + k)
        for b in range(batch) for r in range(per) for k in range(2 * batch)
    ]


def store_steps(size, batch):
    return [
        (e // 2, b * 2 + e % 2, b * 2 * size + e) for b in range(batch) for e in range(2 * size)
    ]


def gather_kernel(layer, count, steps, *refs):
    table, x = refs[:2]
    shards_in, refs = refs[2 : 2 + count], refs[2 + count :]
    moved, fulls, refs = refs[0], refs[1 : 1 + count], refs[1 + count :]
    held, refs = refs[:count], refs[count:]
    mid, turned, send, recv, pass_send, pass_recv, local, x_send, x_recv, x_local = refs
    pending = []
    jobs = [
        Gather(
            shards_in[i].at[layer] if i else shards_in[i], held[i], fulls[i], send.at[i], recv.at[i],
            pass_send.at[i], pass_recv.at[i], local.at[i], pending,
        )
        for i in range(count)
    ]
    for job in jobs:
        job.load()
    greet(lax.axis_size("ctx"), lax.axis_size("fsdp"))
    shuffle = Shuffle(x, mid, turned, moved, table, x_send, x_recv, x_local, pending, steps)
    for t in range(count + 2):
        if t < count:
            jobs[t].first()
        if t == 0:
            shuffle.first()
        if 0 <= t - 1 < count:
            jobs[t - 1].second()
        if t == 2:
            shuffle.second()
        if 0 <= t - 2 < count:
            jobs[t - 2].third()
    shuffle.third()
    for wait in pending:
        wait()


def gather_all(x, table, steps, layer, packed, weights):
    size, groups = lax.axis_size("ctx"), lax.axis_size("fsdp")
    shards_in = [packed] + list(weights)
    count = len(shards_in)
    dma = pltpu.SemaphoreType.DMA
    vmem, smem = pl.BlockSpec(memory_space=pltpu.VMEM), pl.BlockSpec(memory_space=pltpu.SMEM)
    hbm = pl.BlockSpec(memory_space=pl.ANY)
    outs = pl.pallas_call(
        partial(gather_kernel, layer, count, steps),
        name="gather_weights",
        in_specs=[smem, vmem] + [hbm] * count,
        out_specs=[vmem] + [hbm] * count,
        out_shape=[jax.ShapeDtypeStruct(x.shape, x.dtype)]
        + [jax.ShapeDtypeStruct((groups * s.shape[-2], s.shape[-1]), s.dtype) for s in shards_in],
        scratch_shapes=[pltpu.VMEM(s.shape[-2:], s.dtype) for s in shards_in]
        + [pltpu.VMEM(x.shape, x.dtype)] * 2
        + [dma((count, Gather.flows))] * 4
        + [dma((count, 2)), dma((2, size - 1)), dma((2, size - 1)), dma((2,))],
        compiler_params=pltpu.CompilerParams(collective_id=0, has_side_effects=True),
    )(table, x, *shards_in)
    return outs[0], outs[1], outs[2:]


def add_rows(dst, src, rows, out=None):
    out = dst if out is None else out
    block = 16 if rows % 16 == 0 else 8

    def step(i, _):
        span = pl.ds(pl.multiple_of(i * block, block), block)
        out[span, :] = dst[span, :] + src[span, :]
        return 0

    lax.fori_loop(0, rows // block, step, 0)


class Reduce:
    def __init__(self, grad, total, acc, pair, half, quarter, column, sems, pending):
        self.grad, self.total, self.pending = grad, total, pending
        self.acc, self.pair, self.half, self.quarter, self.column = acc, pair, half, quarter, column
        self.sems = sems
        self.rows = total.shape[0]
        self.f, self.c = lax.axis_index("fsdp"), lax.axis_index("ctx")
        self.core = self.c % 2
        self.sibling = self.c + 1 - 2 * self.core
        self.level = self.c // 2
        self.levels = lax.axis_size("ctx") // 2

    def go(self, src, dst, number, **device):
        copy = remote(src, dst, self.sems.at[0, number], self.sems.at[1, number], **device)
        copy.start()
        self.pending.append(copy.wait_send)

    def landed(self, dst, number, **device):
        remote(dst, dst, self.sems.at[0, number], self.sems.at[1, number], **device).wait_recv()

    def step0(self):
        h = self.rows // 2
        self.loads = []
        for owner in range(4):
            self.go(
                self.grad.at[pl.ds(owner * self.rows + (1 - self.core) * h, h), :],
                self.pair.at[owner], owner, ctx=self.sibling,
            )
            copy = pltpu.make_async_copy(
                self.grad.at[pl.ds(owner * self.rows + self.core * h, h), :],
                self.acc.at[owner], self.sems.at[0, 4 + owner],
            )
            copy.start()
            self.loads.append(copy.wait)

    def step1(self):
        for owner in range(4):
            self.loads[owner]()
            self.landed(self.pair.at[owner], owner, ctx=self.sibling)
            add_rows(self.acc.at[owner], self.pair.at[owner], self.rows // 2)
        s = self.rows // 4
        for q, d1, d2 in COLOURS:
            to = far(self.f, d2)
            for k, owner in enumerate((to, far(to, d1))):
                self.go(self.acc.at[owner, pl.ds(q * s, s), :], self.half.at[q, k], 8 + 2 * q + k, fsdp=to)

    def step2(self):
        s = self.rows // 4
        for q, d1, d2 in COLOURS:
            come = far(self.f, d2)
            for k, owner in ((1, far(self.f, d1)), (0, self.f)):
                self.landed(self.half.at[q, k], 8 + 2 * q + k, fsdp=come)
                add_rows(self.acc.at[owner, pl.ds(q * s, s), :], self.half.at[q, k], s)
                if k == 1:
                    self.go(
                        self.acc.at[owner, pl.ds(q * s, s), :], self.quarter.at[q], 12 + q, fsdp=owner
                    )

    def step3(self):
        s = self.rows // 4
        for q, d1, d2 in COLOURS:
            self.landed(self.quarter.at[q], 12 + q, fsdp=far(self.f, d1))
            add_rows(self.acc.at[self.f, pl.ds(q * s, s), :], self.quarter.at[q], s)
        self.chain(0)

    def final(self, core, q):
        s = self.rows // 4
        return self.total.at[pl.ds(core * 2 * s + q * s, s), :]

    def go_if(self, here, src, dst, number, device):
        @pl.when(here)
        def _():
            remote(src, dst, self.sems.at[0, number], self.sems.at[1, number], ctx=device).start()

        def wait():
            @pl.when(here)
            def _():
                remote(src, dst, self.sems.at[0, number], self.sems.at[1, number], ctx=device).wait_send()

        self.pending.append(wait)

    def chain(self, hop):
        s, last = self.rows // 4, self.levels - 1
        for q in range(2):
            place = self.level if q == 0 else last - self.level
            ahead = self.c + 2 if q == 0 else self.c - 2
            behind = self.c - 2 if q == 0 else self.c + 2
            here = place == hop
            acc, column = self.acc.at[self.f, pl.ds(q * s, s), :], self.column.at[q]
            if hop > 0:

                @pl.when(here)
                def _():
                    self.landed(column, 14 + q, ctx=behind)
                    add_rows(acc, column, s, self.final(self.core, q) if hop == last else acc)

            if hop < last:
                self.go_if(here, acc, column, 14 + q, ahead)
            else:
                done = self.final(self.core, q)
                self.go_if(here, done, done, 16 + q, behind)
                self.go_if(here, done, done, 18 + q, self.sibling)

    def back(self, hop):
        last = self.levels - 1
        for q in range(2):
            place = last - self.level if q == 0 else self.level
            ahead = self.c + 2 if q == 0 else self.c - 2
            behind = self.c - 2 if q == 0 else self.c + 2
            here = place == hop
            done = self.final(self.core, q)

            @pl.when(here)
            def _():
                self.landed(done, 16 + q, ctx=ahead)

            if hop < last:
                self.go_if(here, done, done, 16 + q, behind)
            self.go_if(here, done, done, 18 + q, self.sibling)

    def stages(self):
        last = self.levels - 1
        steps = [self.step0, self.step1, self.step2, self.step3]
        steps += [partial(self.chain, hop) for hop in range(1, last + 1)]
        steps += [partial(self.back, hop) for hop in range(1, last + 1)]
        return steps + [self.finish]

    def finish(self):
        for q in range(2):
            self.landed(self.final(1 - self.core, q), 18 + q, ctx=self.sibling)


def reduce_kernel(count, steps, *refs):
    table, x = refs[:2]
    grads, refs = refs[2 : 2 + count], refs[2 + count :]
    moved, totals, refs = refs[0], refs[1 : 1 + count], refs[1 + count :]
    mid, turned, x_send, x_recv, x_local, sems = refs[:6]
    buffers = refs[6:]
    greet(lax.axis_size("ctx"), lax.axis_size("fsdp"))
    pending = []
    jobs = [
        Reduce(grads[i], totals[i], *buffers[5 * i : 5 * i + 5], sems.at[i], pending) for i in range(count)
    ]
    shuffle = Shuffle(x, mid, turned, moved, table, x_send, x_recv, x_local, pending, steps)
    stages = [job.stages() for job in jobs]
    depth = len(stages[0])
    for t in range(count + depth - 1):
        if t == 1:
            shuffle.first()
        for stage in range(depth):
            if 0 <= t - stage < count:
                stages[t - stage][stage]()
        if t == 4:
            shuffle.second()
    shuffle.third()
    for wait in pending:
        wait()


def reduce_all(x, table, steps, grads):
    size, groups = lax.axis_size("ctx"), lax.axis_size("fsdp")
    count = len(grads)
    dma = pltpu.SemaphoreType.DMA
    vmem, smem = pl.BlockSpec(memory_space=pltpu.VMEM), pl.BlockSpec(memory_space=pltpu.SMEM)
    buffers = []
    for g in grads:
        rows, width = g.shape[0] // groups, g.shape[1]
        buffers += [
            pltpu.VMEM((groups, rows // 2, width), BF),
            pltpu.VMEM((groups, rows // 2, width), BF),
            pltpu.VMEM((2, 2, rows // 4, width), BF),
            pltpu.VMEM((2, rows // 4, width), BF),
            pltpu.VMEM((2, rows // 4, width), BF),
        ]
    outs = pl.pallas_call(
        partial(reduce_kernel, count, steps),
        name="reduce_gradients",
        in_specs=[smem, vmem] + [pl.BlockSpec(memory_space=pl.ANY)] * count,
        out_specs=[vmem] + [vmem] * count,
        out_shape=[jax.ShapeDtypeStruct(x.shape, x.dtype)]
        + [jax.ShapeDtypeStruct((g.shape[0] // groups, g.shape[1]), BF) for g in grads],
        scratch_shapes=[pltpu.VMEM(x.shape, x.dtype)] * 2
        + [dma((2, size - 1)), dma((2, size - 1)), dma((2,)), dma((count, 2, 20))]
        + buffers,
        compiler_params=pltpu.CompilerParams(
            collective_id=1, has_side_effects=True, vmem_limit_bytes=67_043_328
        ),
    )(table, x, *grads)
    return outs[0], outs[1:]


def lanes(rows):
    return lax.broadcasted_iota(jnp.int32, (rows, 2 * HD), 1) < HD


def halves(x):
    low = lanes(x.shape[0])
    zero = jnp.zeros_like(x)
    return jnp.where(low, x, zero), jnp.where(low, zero, x)


def write_masks(own_ref, past_ref, seg_q, seg_own, seg_past, turned):
    n, m = own_ref.shape
    first = lax.broadcasted_iota(jnp.int32, (n, m), 0)
    second = lax.broadcasted_iota(jnp.int32, (n, m), 1)
    order = first <= second if turned else second <= first
    own_ref[...] = jnp.where((seg_q == seg_own) & order, 0.0, NEG)
    past_ref[...] = jnp.where(seg_q == seg_past, 0.0, NEG)


def row_blocks(rows, block, body):
    def step(i, _):
        body(pl.ds(pl.multiple_of(i * block, block), block))
        return 0

    lax.fori_loop(0, rows // block, step, 0)


def column_blocks(start, stop, block, body):
    def step(i, _):
        body(pl.ds(pl.multiple_of(start + i * block, block), block))
        return 0

    lax.fori_loop(0, (stop - start) // block, step, 0)


def load_all(pairs, sems):
    waits = []
    for n, (src, dst) in enumerate(pairs):
        copy = pltpu.make_async_copy(src, dst, sems.at[n])
        copy.start()
        waits.append(copy.wait)
    return waits


def place_in_run(runs):
    c = lax.axis_index("ctx")
    return c, c % runs == 0, c % runs == runs - 1


def send_rows(src, dst, sems, device, sends, receives):
    @pl.when(sends)
    def _():
        remote(src, dst, sems.at[0], sems.at[1], ctx=device).start()

    def sent():
        @pl.when(sends)
        def _():
            remote(src, dst, sems.at[0], sems.at[1], ctx=device).wait_send()

    def landed():
        @pl.when(receives)
        def _():
            remote(src, dst, sems.at[0], sems.at[1], ctx=device).wait_recv()

    return sent, landed


def attend_pair(at, q_ref, kv_ref, past_ref, own_mask, past_mask, o_ref, lse_ref, width):
    rows = q_ref.shape[0]
    cols = pl.ds(at, 2 * HD)
    k_cols, v_cols = pl.ds(pl.multiple_of(width + at, 2 * HD), 2 * HD), pl.ds(
        pl.multiple_of(2 * width + at, 2 * HD), 2 * HD
    )
    past_v = pl.ds(pl.multiple_of(width + at, 2 * HD), 2 * HD)
    one = jnp.ones((), BF)
    low_k = lanes(rows)
    v_own, v_past = kv_ref[:, v_cols], past_ref[:, past_v]
    ones_own = (jnp.where(low_k, v_own, one), jnp.where(low_k, one, v_own))
    ones_past = (jnp.where(low_k, v_past, one), jnp.where(low_k, one, v_past))
    for r0 in range(0, rows, QT):
        tile, own = slice(r0, r0 + QT), slice(0, r0 + QT)
        past = slice(r0, rows)
        low = lanes(QT)
        k_own, k_past = kv_ref[own, k_cols], past_ref[past, cols]
        results, tops = [], []
        for j, q in enumerate(halves(q_ref[tile, cols] * jnp.asarray(HD**-0.5, BF))):
            s_own = dot_t(q, k_own) + own_mask[tile, own]
            s_past = dot_t(q, k_past) + past_mask[tile, past]
            top = jnp.maximum(
                jnp.max(s_own, axis=-1, keepdims=True), jnp.max(s_past, axis=-1, keepdims=True)
            )
            results.append(
                dot_n(jnp.exp(s_own - top).astype(BF), ones_own[j][own])
                + dot_n(jnp.exp(s_past - top).astype(BF), ones_past[j][past])
            )
            tops.append(top)
        total = pltpu.roll(jnp.where(low, results[1], results[0]), HD, 1)
        o_ref[tile, cols] = (jnp.where(low, results[0], results[1]) / total).astype(BF)
        lse_ref[tile, cols] = jnp.where(low, tops[0], tops[1]) + jnp.log(total)


def forward_kernel(runs, jobs_of, *refs):
    u_ref, vec_ref, bias_up, sq, so, sp, w_qkv, w_out, w_up, w_down = refs[:10]
    refs = refs[10:]
    gain1, bias_out, gain2, bias_down = (vec_ref.at[i : i + 1, :] for i in (0, 3, 4, 5))
    guests, refs = refs[: jobs_of.inputs], refs[jobs_of.inputs :]
    u2_ref, a1_ref, a1p_ref, qkv_ref, past_ref, mixed_ref, lse_ref, u1_ref, z_ref = refs[:9]
    refs = refs[9:]
    results, refs = refs[: jobs_of.outputs], refs[jobs_of.outputs :]
    (vqkv, vout, vup, vdown, own_mask, past_mask, a2_ref, z_buf, load_sems, halo_sems, z_sems) = refs[:11]
    rows, width = u_ref.shape
    hidden = z_ref.shape[1]
    waits = load_all(((w_qkv, vqkv), (w_out, vout), (w_up, vup), (w_down, vdown)), load_sems)

    def norm_rows(span):
        u = u_ref[span, :]
        a1_ref[span, :] = (u * inverse_rms(u) * gain1[...]).astype(BF)

    row_blocks(rows, 128, norm_rows)
    greet(lax.axis_size("ctx"), lax.axis_size("fsdp"))
    c, is_first, is_last = place_in_run(runs)
    sent, landed = send_rows(
        a1_ref, a1p_ref, halo_sems, c + 1, jnp.logical_not(is_last), jnp.logical_not(is_first)
    )
    jobs = jobs_of(guests, results, refs[11:])
    jobs.start()
    waits[0]()

    def project(i, _):
        span = pl.ds(pl.multiple_of(i * 256, 256), 256)
        src = pl.ds(pl.multiple_of(i * 256 % width, 256), 256)
        third = i * 256 // width
        bias = jnp.where(third == 0, vec_ref[1:2, src], jnp.where(third == 2, vec_ref[2:3, src], 0.0))
        qkv_ref[:, span] = (dot_n(a1_ref[...], vqkv[:, span]) + bias).astype(BF)
        return 0

    lax.fori_loop(0, 3 * width // 256, project, 0)
    write_masks(own_mask, past_mask, sq[...], so[...], sp[...], False)
    landed()

    @pl.when(is_first)
    def _():
        a1p_ref[...] = jnp.zeros_like(a1p_ref)

    def project_past(i, _):
        src = pl.ds(pl.multiple_of(width + i * 256, 256), 256)
        bias = jnp.where(
            i * 256 // width == 1, vec_ref[2:3, pl.ds(pl.multiple_of(i * 256 % width, 256), 256)], 0.0
        )
        y = dot_n(a1p_ref[...], vqkv[:, src]) + bias
        past_ref[:, pl.ds(pl.multiple_of(i * 256, 256), 256)] = y.astype(BF)
        return 0

    lax.fori_loop(0, 2 * width // 256, project_past, 0)

    def pair(i, _):
        attend_pair(
            pl.multiple_of(i * 2 * HD, 2 * HD), qkv_ref, qkv_ref, past_ref, own_mask, past_mask,
            mixed_ref, lse_ref, width,
        )
        return 0

    lax.fori_loop(0, width // (2 * HD), pair, 0)
    waits[1]()

    def middle(span):
        y = dot_n(mixed_ref[span, :], vout[...]) + bias_out[...]
        u1 = u_ref[span, :] + off_mean(y)
        u1_ref[span, :] = u1
        a2_ref[span, :] = (u1 * inverse_rms(u1) * gain2[...]).astype(BF)
        u2_ref[span, :] = u1 + bias_down[...] - jnp.mean(bias_down[...], axis=-1, keepdims=True)

    row_blocks(rows, 256, middle)
    waits[2]()
    waits[3]()
    block = 512

    def z_copy(span, i):
        return pltpu.make_async_copy(z_buf.at[:, span], z_ref.at[:, span], z_sems.at[i])

    for i in range(hidden // block):
        span = pl.ds(i * block, block)
        z = dot_n(a2_ref[...], vup[:, span]) + bias_up[:, span]
        z_buf[:, span] = z
        z_copy(span, i).start()
        act = jax.nn.gelu(z, approximate=True).astype(BF)
        part = dot_n(act, vdown[span, :])
        u2_ref[...] += off_mean(part)
    jobs.finish()
    for i in range(hidden // block):
        z_copy(pl.ds(i * block, block), i).wait()
    sent()


class NoJobs:
    inputs = outputs = 0
    arrays, shapes, scratch = (), (), ()

    def __call__(self, guests, results, scratch):
        return self

    def start(self):
        pass

    def hook(self, number):
        pass

    def finish(self):
        pass


class GatherJobs:
    def __init__(self, layer, shards_in):
        groups = lax.axis_size("fsdp")
        self.layer = layer
        self.inputs = self.outputs = len(shards_in)
        self.arrays = tuple(shards_in)
        self.shapes = tuple(
            jax.ShapeDtypeStruct((groups * s.shape[1], s.shape[2]), s.dtype) for s in shards_in
        )
        dma, n = pltpu.SemaphoreType.DMA, len(shards_in)
        self.scratch = (*(pltpu.VMEM(s.shape[1:], s.dtype) for s in shards_in),)
        self.scratch += (dma((n, Gather.flows)),) * 4 + (dma((n, 2)),)

    def __call__(self, guests, results, scratch):
        n = self.inputs
        send, recv, pass_send, pass_recv, local = scratch[n:]
        self.pending = []
        self.jobs = [
            Gather(
                guests[i].at[self.layer], scratch[i], results[i], send.at[i], recv.at[i], pass_send.at[i],
                pass_recv.at[i], local.at[i], self.pending,
            )
            for i in range(n)
        ]
        return self

    def start(self):
        for job in self.jobs:
            job.load()
        for job in self.jobs:
            job.first()

    def hook(self, number):
        pass

    def finish(self):
        for job in self.jobs:
            job.second()
        for job in self.jobs:
            job.third()
        for wait in self.pending:
            wait()


def fused_forward(u, vec, bias_up, matrices, segs, runs, jobs, number):
    w_qkv, w_out, w_up, w_down = matrices
    rows, width = u.shape
    hidden = w_up.shape[1]
    dma = pltpu.SemaphoreType.DMA
    vmem, hbm = pl.BlockSpec(memory_space=pltpu.VMEM), pl.BlockSpec(memory_space=pl.ANY)
    shape = jax.ShapeDtypeStruct
    outs = pl.pallas_call(
        partial(forward_kernel, runs, jobs),
        name=f"layer_forward_{number}",
        in_specs=[vmem] * 6 + [hbm] * 4 + [hbm] * jobs.inputs,
        out_specs=[vmem] * 8 + [hbm] + [hbm] * jobs.outputs,
        out_shape=[
            shape((rows, width), F32), shape((rows, width), BF), shape((rows, width), BF),
            shape((rows, 3 * width), BF), shape((rows, 2 * width), BF), shape((rows, width), BF),
            shape((rows, width), F32), shape((rows, width), F32), shape((rows, hidden), F32),
            *jobs.shapes,
        ],
        scratch_shapes=[
            *(pltpu.VMEM(x.shape, BF) for x in (w_qkv, w_out, w_up, w_down)),
            pltpu.VMEM((rows, rows), F32), pltpu.VMEM((rows, rows), F32),
            pltpu.VMEM((rows, width), BF), pltpu.VMEM((rows, hidden), F32),
            dma((4,)), dma((2,)), dma((hidden // 512,)), *jobs.scratch,
        ],
        compiler_params=pltpu.CompilerParams(
            collective_id=2 + number, has_side_effects=True, vmem_limit_bytes=67_043_328
        ),
    )(u, vec, bias_up, *segs, w_qkv, w_out, w_up, w_down, *jobs.arrays)
    return outs[0], outs[1:9], outs[9:]


def gelu_parts(z):
    c, d = 0.7978845608028654, 0.044715
    square = z * z
    t = jnp.tanh(c * z * (1.0 + d * square))
    half = 0.5 * (1.0 + t)
    return z * half, half + 0.5 * z * (1.0 - t * t) * (c * (1.0 + 3.0 * d * square))


def norm_back_rows(d_normed, u, gain):
    r = inverse_rms(u)
    n = u * r
    e = d_normed * gain
    du = r * (e - n * jnp.mean(e * n, axis=-1, keepdims=True))
    return du, jnp.sum(d_normed * n, axis=0, keepdims=True)


def attend_pair_back(at, q_ref, past_ref, do_ref, o_ref, lse_ref, own_mask, past_mask, dqkv_ref, dpast_ref, sums, width):
    rows = do_ref.shape[0]
    cols = pl.ds(at, 2 * HD)
    k_cols = pl.ds(pl.multiple_of(width + at, 2 * HD), 2 * HD)
    v_cols = pl.ds(pl.multiple_of(2 * width + at, 2 * HD), 2 * HD)
    dk_ref, dv_ref, dkp_ref, dvp_ref = sums
    for ref in sums:
        ref[...] = jnp.zeros_like(ref)
    do = do_ref[:, cols]
    lse_rows = lse_ref[:, cols].T
    inner_all = (do.astype(F32) * o_ref[:, cols].astype(F32)).T
    inner_rows = [jnp.sum(inner_all[j * HD : (j + 1) * HD], axis=0, keepdims=True) for j in range(2)]
    low = lanes(QT)
    scale = HD**-0.5
    for r0 in range(0, rows, QT):
        tile, own, past = slice(r0, r0 + QT), slice(0, r0 + QT), slice(r0, rows)
        qs = halves(q_ref[tile, cols] * jnp.asarray(scale, BF))
        dos = halves(do[tile])
        dqs = []
        for j in range(2):
            lse = lse_rows[j * HD : j * HD + 1, tile]
            inner = inner_rows[j][:, tile]
            dq = None
            for k, v, mask, dk_sum, dv_sum, span in (
                (q_ref[own, k_cols], q_ref[own, v_cols], own_mask, dk_ref, dv_ref, own),
                (past_ref[past, cols], past_ref[past, k_cols], past_mask, dkp_ref, dvp_ref, past),
            ):
                p = jnp.exp(dot_t(k, qs[j]) + mask[span, tile] - lse)
                ds = (p * (dot_t(v, dos[j]) - inner)).astype(BF)
                dk_sum[span, :] += dot_n(ds, qs[j])
                dv_sum[span, :] += dot_n(p.astype(BF), dos[j])
                part = dot_l(ds, k)
                dq = part if dq is None else dq + part
            dqs.append(dq)
        dqkv_ref[tile, cols] = (jnp.where(low, dqs[0], dqs[1]) * scale).astype(BF)
    dqkv_ref[:, k_cols] = dk_ref[...].astype(BF)
    dqkv_ref[:, v_cols] = dv_ref[...].astype(BF)
    dpast_ref[:, cols] = dkp_ref[...].astype(BF)
    dpast_ref[:, k_cols] = dvp_ref[...].astype(BF)


def backward_kernel(runs, jobs_of, *refs):
    (g_in, u_ref, a1_ref, a1p_ref, qkv_ref, past_ref, mixed_ref, lse_ref, u1_ref, vec_ref,
     sq, so, sp, z_ref, w_qkv, w_out, w_up, w_down) = refs[:18]
    refs = refs[18:]
    gain1, gain2 = vec_ref.at[0:1, :], vec_ref.at[4:5, :]
    guests, refs = refs[: jobs_of.inputs], refs[jobs_of.inputs :]
    g_ref, dvec, dbias_up, dw_qkv, dw_out, dw_up, dw_down = refs[:7]
    refs = refs[7:]
    dgain1, dbias_q, dbias_v, dbias_out, dgain2, dbias_down = (dvec.at[i : i + 1, :] for i in range(6))
    results, refs = refs[: jobs_of.outputs], refs[jobs_of.outputs :]
    (vqkv, vout, vup, vdown, own_mask, past_mask, a2_ref, dy_ref, da_ref, dmix_ref, dqkv_ref, dpast_ref,
     back_ref, come_ref, z_buf, sum0, sum1, sum2, sum3, load_sems, z_sems, out_sems, halo_sems) = refs[:23]
    rows, width = u_ref.shape
    hidden = z_ref.shape[1]
    block = z_buf.shape[2]
    waits = load_all(((w_down, vdown), (w_up, vup), (w_out, vout), (w_qkv, vqkv)), load_sems)

    def z_copy(i, slot):
        span = pl.ds(pl.multiple_of(i * block, block), block)
        return pltpu.make_async_copy(z_ref.at[:, span], z_buf.at[slot], z_sems.at[slot])

    z_copy(0, 0).start()
    greet(lax.axis_size("ctx"), lax.axis_size("fsdp"))
    jobs = jobs_of(guests, results, refs[23:])
    jobs.start()
    for ref in (dvec, da_ref):
        ref[...] = jnp.zeros_like(ref)

    def head_rows(span):
        dy2 = off_mean(g_in[span, :]).astype(BF)
        dy_ref[span, :] = dy2
        dbias_down[...] += jnp.sum(dy2.astype(F32), axis=0, keepdims=True)
        u1 = u1_ref[span, :]
        a2_ref[span, :] = (u1 * inverse_rms(u1) * gain2[...]).astype(BF)

    row_blocks(rows, 128, head_rows)
    waits[0]()
    waits[1]()
    blocks = hidden // block

    def mlp(i, _):
        slot = i % 2
        z_copy(i, slot).wait()

        @pl.when(i + 1 < blocks)
        def _():
            z_copy(i + 1, 1 - slot).start()

        span = pl.ds(pl.multiple_of(i * block, block), block)
        value, slope = gelu_parts(z_buf[slot])
        dz = dot_t(dy_ref[...], vdown[span, :]) * slope
        dz = dz.astype(BF)
        dbias_up[:, span] = jnp.sum(dz.astype(F32), axis=0, keepdims=True)
        vdown[span, :] = dot_l(value.astype(BF), dy_ref[...]).astype(BF)
        da_ref[...] += dot_t(dz, vup[:, span])
        vup[:, span] = dot_l(a2_ref[...], dz).astype(BF)
        return 0

    lax.fori_loop(0, blocks, mlp, 0)
    stores = [
        pltpu.make_async_copy(src, dst, out_sems.at[n])
        for n, (src, dst) in enumerate(((vdown, dw_down), (vup, dw_up), (vout, dw_out), (vqkv, dw_qkv)))
    ]
    stores[0].start()
    stores[1].start()
    jobs.hook(0)

    def middle(span):
        du, part = norm_back_rows(da_ref[span, :], u1_ref[span, :], gain2[...])
        dgain2[...] += part
        g = g_in[span, :] + du
        g_ref[span, :] = g
        dy = off_mean(g).astype(BF)
        dy_ref[span, :] = dy
        dbias_out[...] += jnp.sum(dy.astype(F32), axis=0, keepdims=True)

    row_blocks(rows, 128, middle)
    waits[2]()

    def mixed_back(span):
        dmix_ref[:, span] = dot_t(dy_ref[...], vout[span, :]).astype(BF)

    column_blocks(0, width, 256, mixed_back)

    def out_back(span):
        vout[span, :] = dot_l(mixed_ref[:, span], dy_ref[...]).astype(BF)

    column_blocks(0, width, 256, out_back)
    stores[2].start()
    write_masks(own_mask, past_mask, sq[...], so[...], sp[...], True)

    def pair(i, _):
        attend_pair_back(
            pl.multiple_of(i * 2 * HD, 2 * HD), qkv_ref, past_ref, dmix_ref, mixed_ref, lse_ref,
            own_mask, past_mask, dqkv_ref, dpast_ref, (sum0, sum1, sum2, sum3), width,
        )
        return 0

    lax.fori_loop(0, width // (2 * HD), pair, 0)
    waits[3]()
    back_ref[...] = dot_t(dpast_ref[...], vqkv[:, width:]).astype(BF)
    c, is_first, is_last = place_in_run(runs)
    sent, landed = send_rows(
        back_ref, come_ref, halo_sems, c - 1, jnp.logical_not(is_first), jnp.logical_not(is_last)
    )
    jobs.hook(1)
    da_ref[...] = dot_t(dqkv_ref[...], vqkv[...])

    def qkv_back(span):
        d = dqkv_ref[:, span]
        dbias_q[:, span] = jnp.sum(d.astype(F32), axis=0, keepdims=True)
        vqkv[:, span] = dot_l(a1_ref[...], d).astype(BF)

    column_blocks(0, width, 256, qkv_back)

    def kv_back(i, _):
        span = pl.ds(pl.multiple_of(width + i * 256, 256), 256)
        d, dp = dqkv_ref[:, span], dpast_ref[:, pl.ds(pl.multiple_of(i * 256, 256), 256)]
        dbias_v[:, pl.ds(pl.multiple_of(i * 256 % width, 256), 256)] = jnp.sum(
            d.astype(F32), axis=0, keepdims=True
        ) + jnp.sum(dp.astype(F32), axis=0, keepdims=True)
        vqkv[:, span] = (dot_l(a1_ref[...], d) + dot_l(a1p_ref[...], dp)).astype(BF)
        return 0

    lax.fori_loop(0, 2 * width // 256, kv_back, 0)
    stores[3].start()
    landed()

    @pl.when(is_last)
    def _():
        come_ref[...] = jnp.zeros_like(come_ref)

    def tail(span):
        d = da_ref[span, :] + come_ref[span, :].astype(F32)
        du, part = norm_back_rows(d, u_ref[span, :], gain1[...])
        dgain1[...] += part
        g_ref[span, :] = g_ref[span, :] + du

    row_blocks(rows, 128, tail)
    jobs.finish()
    for store in stores:
        store.wait()
    sent()


def fused_backward(g, u, saved, vec, matrices, segs, runs, jobs, number):
    w_qkv, w_out, w_up, w_down = matrices
    a1, a1p, qkv, past, mixed, lse, u1, z = saved
    rows, width = u.shape
    hidden = w_up.shape[1]
    seg_col, seg_row, seg_past = segs
    dma = pltpu.SemaphoreType.DMA
    vmem, hbm = pl.BlockSpec(memory_space=pltpu.VMEM), pl.BlockSpec(memory_space=pl.ANY)
    shape = jax.ShapeDtypeStruct
    outs = pl.pallas_call(
        partial(backward_kernel, runs, jobs),
        name=f"layer_backward_{number}",
        in_specs=[vmem] * 13 + [hbm] * 5 + [vmem] * jobs.inputs,
        out_specs=[vmem] * 3 + [hbm] * 4 + [vmem] * jobs.outputs,
        out_shape=[
            shape((rows, width), F32), shape((6, width), F32), shape((1, hidden), F32),
            *(shape(x.shape, BF) for x in (w_qkv, w_out, w_up, w_down)), *jobs.shapes,
        ],
        scratch_shapes=[
            *(pltpu.VMEM(x.shape, BF) for x in (w_qkv, w_out, w_up, w_down)),
            pltpu.VMEM((rows, rows), F32), pltpu.VMEM((rows, rows), F32),
            pltpu.VMEM((rows, width), BF), pltpu.VMEM((rows, width), BF), pltpu.VMEM((rows, width), F32),
            pltpu.VMEM((rows, width), BF), pltpu.VMEM((rows, 3 * width), BF),
            pltpu.VMEM((rows, 2 * width), BF), pltpu.VMEM((rows, width), BF), pltpu.VMEM((rows, width), BF),
            pltpu.VMEM((2, rows, 512), F32),
            *(pltpu.VMEM((rows, 2 * HD), F32) for _ in range(4)),
            dma((4,)), dma((2,)), dma((4,)), dma((2,)), *jobs.scratch,
        ],
        compiler_params=pltpu.CompilerParams(
            collective_id=6 + number, has_side_effects=True, vmem_limit_bytes=67_043_328
        ),
    )(
        g, u, a1, a1p, qkv, past, mixed, lse, u1, vec,
        seg_row, seg_col, seg_past.reshape(-1, 1), z, w_qkv, w_out, w_up, w_down, *jobs.arrays,
    )
    return outs[0], outs[1], outs[2], dict(zip(MATRICES, outs[3:7])), outs[7:]


VECTORS = (0, 2, 3, 5, 6, 10)
MATRICES = (1, 4, 7, 9)
LONG = 8


def pad_to(flat, n):
    return jnp.pad(flat, [(0, 0)] * (flat.ndim - 1) + [(0, n - flat.shape[-1])])


def step_kernels(block_input, cotangent, block_order, weights, segs, size, groups, runs):
    batch, _, rows, narrow = block_input.shape
    width, run, block = narrow + 1, batch * rows, rows // 2
    layers = weights[0].shape[0]
    hidden = weights[LONG].shape[1] * groups
    many = len(VECTORS)
    each = layers * (many * width + hidden) // groups
    lines = -(-each // 4096) * 32
    grad_lines = -(-each // 8192) * 64

    blocks = jnp.arange(2 * size, dtype=jnp.int32)
    place = jnp.sum(jnp.where(block_order[None, :] == blocks[:, None], blocks[None, :], 0), axis=1)
    table = jnp.stack(
        [
            jnp.concatenate([place // 2] * batch),
            jnp.concatenate([b * 2 + place % 2 for b in range(batch)]),
        ]
    )
    pad = [(0, 0), (0, 0), (0, 1)]
    both = jnp.concatenate([jnp.pad(block_input[:, 0], pad), jnp.pad(cotangent[:, 0], pad)], axis=2)
    x = both.reshape(batch, 2, size, block // size, 2 * width).transpose(2, 0, 1, 3, 4)
    x = x.reshape(size, 2 * batch, block // size, 2 * width)
    short = jnp.stack([weights[m] for m in VECTORS], axis=1)
    packed = jnp.concatenate([short.reshape(-1), weights[LONG].reshape(-1)])
    packed = pad_to(packed, lines * 128).reshape(lines, 128)
    x, packed, full = gather_all(
        x, table, run_steps(size, batch), 0, packed, [weights[m] for m in MATRICES]
    )
    packed = packed.reshape(groups, lines * 128)
    cut = layers * many * width // groups
    short = packed[:, :cut].reshape(groups, layers * many, width // groups)
    short = short.transpose(1, 0, 2).reshape(layers, many, width).astype(F32)
    long = packed[:, cut:each].reshape(groups, layers, hidden // groups)
    long = long.transpose(1, 0, 2).reshape(layers, 1, hidden).astype(F32)

    both = x.transpose(1, 0, 2, 3).reshape(run, 2 * width).astype(F32)
    h, g = both[:, :width], both[:, width:]
    u = h - jnp.pad(jnp.sum(h, axis=1, keepdims=True), [(0, 0), (width - 1, 0)])
    kept, matrices = [], [full]
    for layer in range(layers):
        more = layer + 1 < layers
        jobs = GatherJobs(layer + 1, [weights[m] for m in MATRICES]) if more else NoJobs()
        u_in = u
        u, saved, full = fused_forward(u, short[layer], long[layer], matrices[layer], segs, runs, jobs, layer)
        kept.append((u_in, saved))
        matrices.append(full)
    dshort, dlong, grads = [None] * layers, [None] * layers, [None] * layers
    for layer in reversed(range(layers)):
        g, dshort[layer], dlong[layer], grads[layer], _ = fused_backward(
            g, *kept[layer], short[layer], matrices[layer], segs, runs, NoJobs(), layer
        )
    both = jnp.concatenate([u.astype(BF), (g - g[:, narrow:]).astype(BF)], axis=1)
    table = jnp.stack(
        [
            jnp.concatenate([b * runs + block_order // (2 * batch) for b in range(batch)]),
            jnp.concatenate([block_order % (2 * batch)] * batch),
        ]
    ).astype(jnp.int32)
    x = both.reshape(2 * batch, size, block // size, 2 * width).transpose(1, 0, 2, 3)
    short = jnp.concatenate(dshort).reshape(layers * many, groups, width // groups)
    long = jnp.concatenate(dlong).reshape(layers, groups, hidden // groups)
    packed = jnp.concatenate(
        [v.transpose(1, 0, 2).reshape(groups, -1).astype(BF) for v in (short, long)], axis=1
    )
    packed = pad_to(packed, grad_lines * 128).reshape(groups * grad_lines, 128)
    order = [(layer, m) for layer in reversed(range(layers)) for m in (9, 7, 4, 1)]
    x, sums = reduce_all(
        x, table, store_steps(size, batch), [grads[layer][m] for layer, m in order] + [packed]
    )
    both = x.reshape(size, batch, 2, block // size, 2 * width).transpose(1, 2, 0, 3, 4)
    both = both.reshape(batch, rows, 2 * width)
    totals = [None] * 11
    found = dict(zip(order, sums))
    for m in MATRICES:
        totals[m] = jnp.stack([found[layer, m] for layer in range(layers)]).astype(F32)
    flat = sums[-1].reshape(-1).astype(F32)
    short = flat[:cut].reshape(layers, many, width // groups)
    for n, m in enumerate(VECTORS):
        totals[m] = short[:, n]
    totals[LONG] = flat[cut:each].reshape(layers, hidden // groups)
    out = both[:, None, :, :narrow]
    d_in = both[:, None, :, width : width + narrow].astype(F32)
    return (out, d_in, *totals)


def step_plain(block_input, cotangent, block_order, weights, segs, size, shift):
    batch, _, rows, narrow = block_input.shape
    layers = weights[0].shape[0]
    both = jnp.concatenate([block_input[:, 0], cotangent[:, 0]], axis=2)
    both = to_runs(jnp.pad(both, [(0, 0), (0, 0), (0, 2)]), block_order, size).astype(F32)
    h, ct = both[:, :narrow], both[:, narrow : 2 * narrow]
    u = jnp.concatenate([h, -jnp.sum(h, axis=1, keepdims=True)], axis=1)
    g = jnp.pad(ct, [(0, 0), (0, 1)])
    full = [lax.all_gather(w, "fsdp", axis=1, tiled=True) for w in weights]
    per_layer = [
        tuple(w[layer] if w.ndim == 3 else w[layer].astype(F32) for w in full) for layer in range(layers)
    ]
    kept = []
    for layer in range(layers):
        u, saved = layer_forward(u, per_layer[layer], segs, shift)
        kept.append(saved)
    grads = [None] * layers
    for layer in reversed(range(layers)):
        g, grads[layer] = layer_backward(g, kept[layer], per_layer[layer], segs, shift)
    out = from_runs(u.astype(BF), block_order, size, batch)[:, None, :, :narrow]
    d_in = from_runs((g - g[:, narrow:]).astype(BF), block_order, size, batch)
    totals = []
    for m in range(11):
        part = jnp.stack([grads[layer][m] for layer in range(layers)]).astype(BF)
        part = lax.psum_scatter(part, "fsdp", scatter_dimension=1, tiled=True)
        totals.append(lax.psum(part, "ctx").astype(F32))
    return (out, d_in[:, None, :, :narrow].astype(F32), *totals)


def shards(block_input, cotangent, segment_ids, block_order, *weights):
    batch, _, rows, _ = block_input.shape
    size, groups = lax.axis_size("ctx"), lax.axis_size("fsdp")
    length = segment_ids.shape[2]
    run = batch * rows
    runs = length // run
    halo_steps = -(-(length // 4) // run)
    halo = halo_steps * run
    index = lax.axis_index("ctx")
    own_seq = lax.dynamic_index_in_dim(segment_ids[:, 0], index // runs, 0, keepdims=False)
    padded = jnp.concatenate([jnp.full((halo,), -1, jnp.int32), own_seq])
    window = lax.dynamic_slice_in_dim(padded, (index % runs) * run, halo + run)
    segs = (window[halo:].reshape(run, 1), window[None, halo:], window[None, :halo])
    if groups == 4 and size == 8 and halo_steps == 1:
        return step_kernels(block_input, cotangent, block_order, weights, segs, size, groups, runs)
    return step_plain(block_input, cotangent, block_order, weights, segs, size, (halo_steps, runs, size))


def solution(mesh):
    rows = P(None, "fsdp", "ctx", None)
    mat, vec = P(None, "fsdp", None), P(None, "fsdp")
    kinds = (vec, mat, vec, vec, mat, vec, vec, mat, vec, mat, vec)
    return jax.shard_map(
        shards,
        mesh=mesh,
        in_specs=(rows, rows, mat, P(), *kinds),
        out_specs=(rows, rows, *kinds),
        check_vma=False,
    )
```

profile of v0, /device:TPU:0, one launch (start us, length us, event | category | flops | bytes accessed | tf_op | source)
XLA Modules:
  0.0 548.2 jit_solution(7543443973219963767)
XLA Ops:
  0.7 0.8 constant_dynamic-slice_fusion
  1.5 0.6 fusion.13
  2.1 0.9 copy.66.refs_3_.refs_11_
  3.0 0.8 select_reduce_fusion
  3.8 0.6 pad_add_fusion.1.refs_0_
  4.4 2.2 copy.58
  6.7 1.2 copy.59
  8.1 1.3 copy.60
  9.6 0.6 fusion.10.refs_2_
  10.2 77.0 %gather_weights.1 = (bf16[8,4,16,1536]{3,2,1,0:T(8,128)(2,1)}, bf16[128,128]{1,0:T(8,128)(2,1)}, bf16[768,2304]{1,0:T(8,128)(2,1)}, bf16[768,768]{1,0:T(8,128)(2...) custom-call(s32[2,32]{1,0:T(2,128)} %pad_add_fusion.1.refs_0_, bf16[8,4,16,1536]{3,2,1,0:T(8,128)(2,1)} %bitcast.101, ...), custom_call_target="tpu_custom_call" | custom-call | tf_op jit(solution)/shard_map/gather_weights/pallas_call | solution.py:487
  87.2 1.8 convert_bitcast_fusion
  89.6 2.0 pad_subtract_fusion
  91.6 0.6 fusion.11
  92.3 0.7 squeeze.45.refs_1_.refs_9_
  93.0 0.6 slice_bitcast_fusion.2
  93.6 0.6 copy.84
  94.2 80.2 %layer_forward_0.1 = (f32[512,768]{1,0:T(8,128)}, bf16[512,768]{1,0:T(8,128)(2,1)}, bf16[512,768]{1,0:T(8,128)(2,1)}, bf16[512,2304]{1,0:T(8,128)(2,1)}, bf16[51...) custom-call(f32[512,768]{1,0:T(8,128)} %get-tuple-element.147.refs_0, ...), custom_call_target="tpu_custom_call" | custom-call | tf_op jit(solution)/shard_map/layer_forward_0/pallas_call | solution.py:968
  174.5 0.8 copy.67
  175.2 0.7 squeeze.48.refs_1_.refs_9_
  175.9 1.3 copy.85
  177.2 35.3 %layer_forward_1.1 = (f32[512,768]{1,0:T(8,128)}, bf16[512,768]{1,0:T(8,128)(2,1)}, bf16[512,768]{1,0:T(8,128)(2,1)}, bf16[512,2304]{1,0:T(8,128)(2,1)}, bf16[51...) custom-call(f32[512,768]{1,0:T(8,128)} %get-tuple-element.71.refs_0_, ...), custom_call_target="tpu_custom_call" | custom-call | tf_op jit(solution)/shard_map/layer_forward_1/pallas_call | solution.py:968
  212.6 1.5 copy.70.refs_12_
  214.1 61.5 %layer_backward_1.1 = (f32[512,768]{1,0:T(8,128)}, f32[6,768]{1,0:T(8,128)}, f32[1,3072]{1,0:T(1,128)}, bf16[768,2304]{1,0:T(8,128)(2,1)}, bf16[768,768]{1,0:T(8...) custom-call(f32[512,768]{1,0:T(8,128)} %get-tuple-element.148.refs_0_, ...), custom_call_target="tpu_custom_call" | custom-call | tf_op jit(solution)/shard_map/layer_backward_1/pallas_call | solution.py:1203
  275.6 59.3 %layer_backward_0.1 = (f32[512,768]{1,0:T(8,128)}, f32[6,768]{1,0:T(8,128)}, f32[1,3072]{1,0:T(1,128)}, bf16[768,2304]{1,0:T(8,128)(2,1)}, bf16[768,768]{1,0:T(8...) custom-call(f32[512,768]{1,0:T(8,128)} %get-tuple-element.85.refs_0_, ...), custom_call_target="tpu_custom_call" | custom-call | tf_op jit(solution)/shard_map/layer_backward_0/pallas_call | solution.py:1203
  334.9 0.7 convert.19
  335.7 0.7 convert.20
  336.7 0.8 convert.21
  337.5 0.7 convert.22
  338.3 0.7 reshape.125.refs_10_
  339.0 1.2 slice_reduce_fusion.1
  340.2 1.6 subtract_convert_fusion
  342.0 1.3 copy.94
  343.4 0.6 pad_add_fusion.refs_0_
  344.0 184.3 %reduce_gradients.1 = (bf16[8,4,16,1536]{3,2,1,0:T(8,128)(2,1)}, bf16[768,768]{1,0:T(8,128)(2,1)}, bf16[192,3072]{1,0:T(8,128)(2,1)}, bf16[192,768]{1,0:T(8,128)...) custom-call(s32[2,32]{1,0:T(2,128)} %pad_add_fusion.refs_0_, ...), custom_call_target="tpu_custom_call" | custom-call | tf_op jit(solution)/shard_map/reduce_gradients/pallas_call | solution.py:689
  528.3 4.3 maximum_convert_fusion.1
  532.6 2.5 maximum_convert_fusion
  535.1 1.1 maximum_convert_fusion.3
  536.2 0.5 copy-done.4
  536.9 2.0 maximum_convert_fusion.2
  539.2 2.8 copy.77
  542.0 1.8 copy.76
  543.8 0.6 copy.96
  544.4 0.6 copy.97
  545.0 0.6 copy.98
  545.6 0.6 copy.99
  546.2 0.6 copy.100
  546.7 0.6 copy.101
  547.3 0.6 reshape.129
  (78 shorter events, 2.4 us)
Async XLA Ops:
  0.6 6.0 %copy-start.6 = (bf16[2,1,256,767]{2,0,3,1:T(2,128)(2,1)S(1)}, bf16[2,1,256,767]{2,0,3,1:T(2,128)(2,1)}, u32[]{:S(2)}) copy-start(bf16[2,1,256,767]{2,0,3,1:T(2,128)(2,1)} %param.16) | copy-start | bytes 2356228
  2.1 1.7 copy-start.9
  8.0 1.4 copy-start.13
  8.0 1.4 copy-start.14
  8.0 1.4 copy-start.15
  8.0 1.4 copy-start.16
  8.1 1.4 copy-start.17
  8.1 1.4 copy-start.18
  8.1 1.5 copy-start.12
  89.6 2.0 copy-start.10
  336.4 5.3 copy-start
  342.0 1.3 copy-start.19
  528.2 4.3 copy-start.2
  528.3 4.3 copy-start.3
  532.5 2.5 copy-start.7
  532.5 2.5 copy-start.8
  535.0 1.6 copy-start.4
  535.1 1.9 copy-start.5
  536.9 2.0 copy-start.1
  542.0 1.8 copy-start.11
where the time goes:
time: 553 us; the launch traced here: 548 us
  Pallas kernels  498 us (90%)
  local copies, waits for them, and re-layouts  27.5 us (5%)
  other arithmetic  21.7 us (4%)
    pallas_call x1, Pallas kernels, reduce_all(): pl.pallas_call(partial(reduce_kernel, count, steps), name='reduce_gradien...  184 us
    pallas_call x2, Pallas kernels, fused_backward(): pl.pallas_call(partial(backward_kernel, runs, jobs), name=f'layer_backwar...  121 us
    pallas_call x2, Pallas kernels, fused_forward(): pl.pallas_call(partial(forward_kernel, runs, jobs), name=f'layer_forward_...  116 us
    pallas_call x1, Pallas kernels, gather_all(): pl.pallas_call(partial(gather_kernel, layer, count, steps), name='gather_...  77 us
    unnamed x58, local copies, waits for them, and re-layouts  14.9 us

commit v1 on v0

--- a/solution.py
+++ b/solution.py
@@ -393,62 +393,88 @@
 
 
 class Shuffle:
-    def __init__(self, x, mid, turned, out, table, send, recv, local, pending, steps):
+    def __init__(self, to_runs_first, x, mid, turned, out, table, sems, pending, batch):
         self.x, self.mid, self.turned, self.out, self.table = x, mid, turned, out, table
-        self.send, self.recv, self.local, self.pending = send, recv, local, pending
-        self.size = x.shape[0]
-        self.steps = steps
-
-    def exchange(self, src, dst, phase):
-        c = lax.axis_index("ctx")
-        landed = []
-        for k in range(1, self.size):
-            to, come = (c + k) % self.size, (c + self.size - k) % self.size
-            send, recv = self.send.at[phase, k - 1], self.recv.at[phase, k - 1]
-            copy = remote(src.at[to], dst.at[c], send, recv, ctx=to)
-            copy.start()
-            self.pending.append(copy.wait_send)
-            landed.append(remote(src.at[to], dst.at[come], send, recv, ctx=come).wait_recv)
-        copy = pltpu.make_async_copy(src.at[c], dst.at[c], self.local.at[phase])
-        copy.start()
-        landed.append(copy.wait)
-        return landed
+        self.sems, self.pending = sems, pending
+        self.size, self.batch = lax.axis_size("ctx"), batch
+        self.wide_first = to_runs_first
+        self.c = lax.axis_index("ctx")
+
+    def exchange(self, src, dst, phase, act):
+        wide = (phase == 0) == self.wide_first
+        n = self.size if wide else self.size // self.batch
+        base, own = (0, self.c) if wide else (self.c // n * n, self.c % n)
+        for k in range(1, n):
+            to, come = (own + k) % n, (own + n - k) % n
+            send, recv = self.sems.at[phase, 0, k], self.sems.at[phase, 1, k]
+            if act == "landed":
+                remote(src.at[to], dst.at[come], send, recv, ctx=base + come).wait_recv()
+                continue
+            copy = remote(src.at[to], dst.at[own], send, recv, ctx=base + to)
+            copy.start() if act == "start" else copy.wait_send()
+        if act != "sent":
+            copy = pltpu.make_async_copy(src.at[own], dst.at[own], self.sems.at[phase, 0, 0])
+            copy.start() if act == "start" else copy.wait()
+
+    def start(self, src, dst, phase):
+        self.exchange(src, dst, phase, "start")
+        self.pending.append(lambda: self.exchange(src, dst, phase, "sent"))
 
     def first(self):
-        self.landed = self.exchange(self.x, self.mid, 0)
+        self.start(self.x, self.mid, 0)
 
     def second(self):
-        for wait in self.landed:
-            wait()
-        for slot, part, entry in self.steps:
-            self.turned[slot, part] = self.mid[self.table[0, entry], self.table[1, entry]]
-        self.landed = self.exchange(self.turned, self.out, 1)
+        self.exchange(self.x, self.mid, 0, "landed")
+        for slot in range(self.turned.shape[0]):
+            for part in range(self.turned.shape[1]):
+                entry = slot * self.turned.shape[1] + part
+                self.turned[slot, part] = self.mid[self.table[0, entry], self.table[1, entry]]
+        self.start(self.turned, self.out, 1)
 
     def third(self):
-        for wait in self.landed:
-            wait()
-
-
-def run_steps(size, batch):
-    per = size // batch
-    return [
-        (b * per + r, k, b * 2 * size + 2 * batch * r + k)
-        for b in range(batch) for r in range(per) for k in range(2 * batch)
-    ]
-
-
-def store_steps(size, batch):
-    return [
-        (e // 2, b * 2 + e % 2, b * 2 * size + e) for b in range(batch) for e in range(2 * size)
-    ]
-
-
-def gather_kernel(layer, count, steps, *refs):
+        self.exchange(self.turned, self.out, 1, "landed")
+
+    @staticmethod
+    def scratch(to_runs_first, size, batch, rows, width):
+        near = size // batch
+        blocks = 2 * batch
+        wide, narrow = (size, 2, rows // blocks // near, width), (near, blocks, rows // blocks // near, width)
+        mid, turned = (wide, narrow) if to_runs_first else (narrow, wide)
+        return [
+            pltpu.VMEM(mid, BF), pltpu.VMEM(turned, BF), pltpu.SemaphoreType.DMA((2, 2, size))
+        ]
+
+
+def for_runs(x, size):
+    batch, rows, width = x.shape
+    near = size // batch
+    x = x.reshape(batch, 2, near, rows // 2 // near, width).transpose(0, 2, 1, 3, 4)
+    return x.reshape(size, 2, rows // 2 // near, width)
+
+
+def of_runs(out):
+    near, blocks, part, width = out.shape
+    return out.transpose(1, 0, 2, 3).reshape(near * blocks * part, width)
+
+
+def for_store(x, near, blocks):
+    rows, width = x.shape
+    return x.reshape(blocks, near, rows // blocks // near, width).transpose(1, 0, 2, 3)
+
+
+def of_store(out, batch):
+    size, _, part, width = out.shape
+    near = size // batch
+    out = out.reshape(batch, near, 2, part, width).transpose(0, 2, 1, 3, 4)
+    return out.reshape(batch, 2 * near * part, width)
+
+
+def gather_kernel(layer, count, batch, *refs):
     table, x = refs[:2]
     shards_in, refs = refs[2 : 2 + count], refs[2 + count :]
     moved, fulls, refs = refs[0], refs[1 : 1 + count], refs[1 + count :]
     held, refs = refs[:count], refs[count:]
-    mid, turned, send, recv, pass_send, pass_recv, local, x_send, x_recv, x_local = refs
+    mid, turned, x_sems, send, recv, pass_send, pass_recv, local = refs
     pending = []
     jobs = [
         Gather(
@@ -460,7 +486,7 @@
     for job in jobs:
         job.load()
     greet(lax.axis_size("ctx"), lax.axis_size("fsdp"))
-    shuffle = Shuffle(x, mid, turned, moved, table, x_send, x_recv, x_local, pending, steps)
+    shuffle = Shuffle(True, x, mid, turned, moved, table, x_sems, pending, batch)
     for t in range(count + 2):
         if t < count:
             jobs[t].first()
@@ -477,24 +503,24 @@
         wait()
 
 
-def gather_all(x, table, steps, layer, packed, weights):
+def gather_all(x, table, layer, batch, packed, weights):
     size, groups = lax.axis_size("ctx"), lax.axis_size("fsdp")
     shards_in = [packed] + list(weights)
     count = len(shards_in)
     dma = pltpu.SemaphoreType.DMA
     vmem, smem = pl.BlockSpec(memory_space=pltpu.VMEM), pl.BlockSpec(memory_space=pltpu.SMEM)
     hbm = pl.BlockSpec(memory_space=pl.ANY)
+    width = x.shape[-1]
+    exchange = Shuffle.scratch(True, size, batch, x.size // width, width)
     outs = pl.pallas_call(
-        partial(gather_kernel, layer, count, steps),
+        partial(gather_kernel, layer, count, batch),
         name="gather_weights",
         in_specs=[smem, vmem] + [hbm] * count,
         out_specs=[vmem] + [hbm] * count,
-        out_shape=[jax.ShapeDtypeStruct(x.shape, x.dtype)]
+        out_shape=[jax.ShapeDtypeStruct(exchange[1].shape, x.dtype)]
         + [jax.ShapeDtypeStruct((groups * s.shape[-2], s.shape[-1]), s.dtype) for s in shards_in],
         scratch_shapes=[pltpu.VMEM(s.shape[-2:], s.dtype) for s in shards_in]
-        + [pltpu.VMEM(x.shape, x.dtype)] * 2
-        + [dma((count, Gather.flows))] * 4
-        + [dma((count, 2)), dma((2, size - 1)), dma((2, size - 1)), dma((2,))],
+        + exchange + [dma((count, Gather.flows))] * 4 + [dma((count, 2))],
         compiler_params=pltpu.CompilerParams(collective_id=0, has_side_effects=True),
     )(table, x, *shards_in)
     return outs[0], outs[1], outs[2:]
@@ -512,194 +538,269 @@
     lax.fori_loop(0, rows // block, step, 0)
 
 
-class Reduce:
-    def __init__(self, grad, total, acc, pair, half, quarter, column, sems, pending):
-        self.grad, self.total, self.pending = grad, total, pending
-        self.acc, self.pair, self.half, self.quarter, self.column = acc, pair, half, quarter, column
-        self.sems = sems
-        self.rows = total.shape[0]
+class Sum:
+    def __init__(self, sems, pending):
+        self.sems, self.pending = sems, pending
         self.f, self.c = lax.axis_index("fsdp"), lax.axis_index("ctx")
         self.core = self.c % 2
         self.sibling = self.c + 1 - 2 * self.core
         self.level = self.c // 2
         self.levels = lax.axis_size("ctx") // 2
 
-    def go(self, src, dst, number, **device):
-        copy = remote(src, dst, self.sems.at[0, number], self.sems.at[1, number], **device)
-        copy.start()
-        self.pending.append(copy.wait_send)
+    def copy(self, src, dst, number, **device):
+        return remote(src, dst, self.sems.at[0, number], self.sems.at[1, number], **device)
+
+    def go(self, make):
+        make().start()
+        self.pending.append(lambda: make().wait_send())
+
+    def go_if(self, here, make):
+        @pl.when(here())
+        def _():
+            make().start()
+
+        def wait():
+            @pl.when(here())
+            def _():
+                make().wait_send()
+
+        self.pending.append(wait)
 
     def landed(self, dst, number, **device):
-        remote(dst, dst, self.sems.at[0, number], self.sems.at[1, number], **device).wait_recv()
+        self.copy(dst, dst, number, **device).wait_recv()
+
+
+class PlaneSum(Sum):
+    def __init__(self, grad, pair, half, quarter, stage, sems, pending):
+        super().__init__(sems, pending)
+        self.grad, self.pair, self.half, self.quarter, self.stage = grad, pair, half, quarter, stage
+        self.rows = grad.shape[0] // 4
+
+    @staticmethod
+    def scratch(shape, in_place):
+        rows, width = shape[0] // 4, shape[1]
+        stage = () if in_place else (pltpu.VMEM((2, rows // 2, width), BF),)
+        return (
+            pltpu.VMEM((4, rows // 2, width), BF), pltpu.VMEM((2, 2, rows // 4, width), BF),
+            pltpu.VMEM((2, rows // 4, width), BF), *stage, pltpu.SemaphoreType.DMA((2, 12)),
+        )
+
+    def part(self, owner, core):
+        h = self.rows // 2
+        return self.grad.at[pl.ds(owner * self.rows + core * h, h), :]
+
+    def acc(self, owner):
+        return self.pair.at[owner] if self.stage is not None else self.part(owner, self.core)
+
+    def colour(self, owner, q):
+        s = self.rows // 4
+        return self.acc(owner).at[pl.ds(q * s, s), :]
+
+    def load(self, owner):
+        slot = owner % 2
+        return pltpu.make_async_copy(
+            self.part(owner, self.core), self.stage.at[slot], self.sems.at[0, 10 + slot]
+        )
 
     def step0(self):
-        h = self.rows // 2
-        self.loads = []
         for owner in range(4):
             self.go(
-                self.grad.at[pl.ds(owner * self.rows + (1 - self.core) * h, h), :],
-                self.pair.at[owner], owner, ctx=self.sibling,
+                lambda owner=owner: self.copy(
+                    self.part(owner, 1 - self.core), self.pair.at[owner], owner, ctx=self.sibling
+                )
             )
-            copy = pltpu.make_async_copy(
-                self.grad.at[pl.ds(owner * self.rows + self.core * h, h), :],
-                self.acc.at[owner], self.sems.at[0, 4 + owner],
-            )
-            copy.start()
-            self.loads.append(copy.wait)
+        if self.stage is not None:
+            self.load(0).start()
 
     def step1(self):
         for owner in range(4):
-            self.loads[owner]()
             self.landed(self.pair.at[owner], owner, ctx=self.sibling)
-            add_rows(self.acc.at[owner], self.pair.at[owner], self.rows // 2)
-        s = self.rows // 4
+            if self.stage is None:
+                add_rows(self.acc(owner), self.pair.at[owner], self.rows // 2)
+            else:
+                self.load(owner).wait()
+                if owner < 3:
+                    self.load(owner + 1).start()
+                add_rows(self.pair.at[owner], self.stage.at[owner % 2], self.rows // 2)
         for q, d1, d2 in COLOURS:
-            to = far(self.f, d2)
-            for k, owner in enumerate((to, far(to, d1))):
-                self.go(self.acc.at[owner, pl.ds(q * s, s), :], self.half.at[q, k], 8 + 2 * q + k, fsdp=to)
+            for k in range(2):
+
+                def make(q=q, d1=d1, d2=d2, k=k):
+                    to = far(self.f, d2)
+                    owner = far(to, d1) if k else to
+                    return self.copy(self.colour(owner, q), self.half.at[q, k], 4 + 2 * q + k, fsdp=to)
+
+                self.go(make)
 
     def step2(self):
         s = self.rows // 4
         for q, d1, d2 in COLOURS:
-            come = far(self.f, d2)
-            for k, owner in ((1, far(self.f, d1)), (0, self.f)):
-                self.landed(self.half.at[q, k], 8 + 2 * q + k, fsdp=come)
-                add_rows(self.acc.at[owner, pl.ds(q * s, s), :], self.half.at[q, k], s)
-                if k == 1:
-                    self.go(
-                        self.acc.at[owner, pl.ds(q * s, s), :], self.quarter.at[q], 12 + q, fsdp=owner
+            for k in (1, 0):
+                owner = far(self.f, d1) if k else self.f
+                self.landed(self.half.at[q, k], 4 + 2 * q + k, fsdp=far(self.f, d2))
+                add_rows(self.colour(owner, q), self.half.at[q, k], s)
+                if k:
+
+                    def make(q=q, d1=d1):
+                        owner = far(self.f, d1)
+                        return self.copy(self.colour(owner, q), self.quarter.at[q], 8 + q, fsdp=owner)
+
+                    self.go(make)
+
+    def step3(self):
+        for q, d1, d2 in COLOURS:
+            self.landed(self.quarter.at[q], 8 + q, fsdp=far(self.f, d1))
+            add_rows(self.colour(self.f, q), self.quarter.at[q], self.rows // 4)
+
+
+class ColumnSum(Sum):
+    def __init__(self, part, column, total, sems, pending):
+        super().__init__(sems, pending)
+        self.part, self.column, self.total = part, column, total
+        self.s = total.shape[0] // 4
+
+    @staticmethod
+    def scratch(rows, width):
+        return pltpu.VMEM((2, rows // 4, width), BF), pltpu.SemaphoreType.DMA((2, 6))
+
+    def final(self, core, q):
+        return self.total.at[pl.ds(core * 2 * self.s + q * self.s, self.s), :]
+
+    def route(self, q):
+        up, down = self.c + 2, self.c - 2
+        return (self.level, up, down) if q == 0 else (self.levels - 1 - self.level, down, up)
+
+    def chain(self, hop):
+        last = self.levels - 1
+        for q in range(2):
+            if hop > 0:
+
+                @pl.when(self.route(q)[0] == hop)
+                def _():
+                    self.landed(self.column.at[q], q, ctx=self.route(q)[2])
+                    acc = self.part(q)
+                    add_rows(
+                        acc, self.column.at[q], self.s, self.final(self.core, q) if hop == last else acc
                     )
 
-    def step3(self):
-        s = self.rows // 4
-        for q, d1, d2 in COLOURS:
-            self.landed(self.quarter.at[q], 12 + q, fsdp=far(self.f, d1))
-            add_rows(self.acc.at[self.f, pl.ds(q * s, s), :], self.quarter.at[q], s)
-        self.chain(0)
-
-    def final(self, core, q):
-        s = self.rows // 4
-        return self.total.at[pl.ds(core * 2 * s + q * s, s), :]
-
-    def go_if(self, here, src, dst, number, device):
-        @pl.when(here)
-        def _():
-            remote(src, dst, self.sems.at[0, number], self.sems.at[1, number], ctx=device).start()
-
-        def wait():
-            @pl.when(here)
-            def _():
-                remote(src, dst, self.sems.at[0, number], self.sems.at[1, number], ctx=device).wait_send()
-
-        self.pending.append(wait)
-
-    def chain(self, hop):
-        s, last = self.rows // 4, self.levels - 1
-        for q in range(2):
-            place = self.level if q == 0 else last - self.level
-            ahead = self.c + 2 if q == 0 else self.c - 2
-            behind = self.c - 2 if q == 0 else self.c + 2
-            here = place == hop
-            acc, column = self.acc.at[self.f, pl.ds(q * s, s), :], self.column.at[q]
-            if hop > 0:
-
-                @pl.when(here)
-                def _():
-                    self.landed(column, 14 + q, ctx=behind)
-                    add_rows(acc, column, s, self.final(self.core, q) if hop == last else acc)
-
             if hop < last:
-                self.go_if(here, acc, column, 14 + q, ahead)
+                self.go_if(
+                    lambda q=q: self.route(q)[0] == hop,
+                    lambda q=q: self.copy(self.part(q), self.column.at[q], q, ctx=self.route(q)[1]),
+                )
             else:
-                done = self.final(self.core, q)
-                self.go_if(here, done, done, 16 + q, behind)
-                self.go_if(here, done, done, 18 + q, self.sibling)
+                self.hand_on(hop, q, True)
+
+    def hand_on(self, place, q, on):
+        here = lambda: self.route(q)[0] == place
+        done = lambda: self.final(self.core, q)
+        if on:
+            self.go_if(here, lambda: self.copy(done(), done(), 2 + q, ctx=self.route(q)[2]))
+        self.go_if(here, lambda: self.copy(done(), done(), 4 + q, ctx=self.sibling))
 
     def back(self, hop):
         last = self.levels - 1
         for q in range(2):
-            place = last - self.level if q == 0 else self.level
-            ahead = self.c + 2 if q == 0 else self.c - 2
-            behind = self.c - 2 if q == 0 else self.c + 2
-            here = place == hop
-            done = self.final(self.core, q)
-
-            @pl.when(here)
+
+            @pl.when(self.route(q)[0] == last - hop)
             def _():
-                self.landed(done, 16 + q, ctx=ahead)
-
-            if hop < last:
-                self.go_if(here, done, done, 16 + q, behind)
-            self.go_if(here, done, done, 18 + q, self.sibling)
-
-    def stages(self):
-        last = self.levels - 1
-        steps = [self.step0, self.step1, self.step2, self.step3]
-        steps += [partial(self.chain, hop) for hop in range(1, last + 1)]
-        steps += [partial(self.back, hop) for hop in range(1, last + 1)]
-        return steps + [self.finish]
+                self.landed(self.final(self.core, q), 2 + q, ctx=self.route(q)[1])
+
+            self.hand_on(last - hop, q, hop < last)
+
+    def hops(self):
+        count = self.levels
+        return [partial(self.chain, hop) for hop in range(count)] + [
+            partial(self.back, hop) for hop in range(1, count)
+        ]
 
     def finish(self):
         for q in range(2):
-            self.landed(self.final(1 - self.core, q), 18 + q, ctx=self.sibling)
-
-
-def reduce_kernel(count, steps, *refs):
-    table, x = refs[:2]
-    grads, refs = refs[2 : 2 + count], refs[2 + count :]
-    moved, totals, refs = refs[0], refs[1 : 1 + count], refs[1 + count :]
-    mid, turned, x_send, x_recv, x_local, sems = refs[:6]
-    buffers = refs[6:]
+            self.landed(self.final(1 - self.core, q), 4 + q, ctx=self.sibling)
+
+
+class Refs:
+    def __init__(self, refs):
+        self.refs, self.at = list(refs), 0
+
+    def take(self, n):
+        self.at += n
+        return self.refs[self.at - n : self.at]
+
+    def one(self):
+        return self.take(1)[0]
+
+
+def reduce_kernel(plan, *refs):
+    ready, batch, planes = plan
+    refs = Refs(refs)
+    table, x = refs.take(2)
+    parts, grads = refs.take(ready), refs.take(planes)
+    moved, totals = refs.one(), refs.take(ready + planes)
+    mid, turned, x_sems = refs.take(3)
+    pending = []
+    jobs = []
+    for i in range(planes):
+        pair, half, quarter, stage, sems = refs.take(5)
+        jobs.append(PlaneSum(grads[i], pair, half, quarter, stage, sems, pending))
+    columns = []
+    for i in range(ready + planes):
+        column, sems = refs.take(2)
+        if i < ready:
+            s = parts[i].shape[0] // 2
+            part = lambda q, i=i, s=s: parts[i].at[pl.ds(q * s, s), :]
+        else:
+            job = jobs[i - ready]
+            part = lambda q, job=job: job.colour(job.f, q)
+        columns.append(ColumnSum(part, column, totals[i], sems, pending))
     greet(lax.axis_size("ctx"), lax.axis_size("fsdp"))
-    pending = []
-    jobs = [
-        Reduce(grads[i], totals[i], *buffers[5 * i : 5 * i + 5], sems.at[i], pending) for i in range(count)
-    ]
-    shuffle = Shuffle(x, mid, turned, moved, table, x_send, x_recv, x_local, pending, steps)
-    stages = [job.stages() for job in jobs]
-    depth = len(stages[0])
-    for t in range(count + depth - 1):
-        if t == 1:
-            shuffle.first()
-        for stage in range(depth):
-            if 0 <= t - stage < count:
-                stages[t - stage][stage]()
-        if t == 4:
+    shuffle = Shuffle(False, x, mid, turned, moved, table, x_sems, pending, batch)
+    lines = [c.hops() for c in columns[:ready]]
+    for job, c in zip(jobs, columns[ready:]):
+        lines.append([job.step0, job.step1, job.step2, job.step3] + c.hops())
+    order = list(range(ready, ready + planes)) + list(range(ready))
+    delay = {n: max(0, k - 1) for k, n in enumerate(order)}
+    for k, n in enumerate(order):
+        delay[n] = k if n >= ready else k - planes
+    shuffle.first()
+    depth = max(len(line) + delay[n] for n, line in enumerate(lines))
+    for t in range(depth):
+        for n in order:
+            if 0 <= t - delay[n] < len(lines[n]):
+                lines[n][t - delay[n]]()
+        if t == 2:
             shuffle.second()
+    for c in columns:
+        c.finish()
     shuffle.third()
     for wait in pending:
         wait()
 
 
-def reduce_all(x, table, steps, grads):
+def reduce_all(x, table, batch, parts, grads):
     size, groups = lax.axis_size("ctx"), lax.axis_size("fsdp")
-    count = len(grads)
-    dma = pltpu.SemaphoreType.DMA
     vmem, smem = pl.BlockSpec(memory_space=pltpu.VMEM), pl.BlockSpec(memory_space=pltpu.SMEM)
-    buffers = []
+    width = x.shape[-1]
+    exchange = Shuffle.scratch(False, size, batch, x.size // width, width)
+    shards_out = [(2 * p.shape[0], p.shape[1]) for p in parts]
+    shards_out += [(g.shape[0] // groups, g.shape[1]) for g in grads]
+    scratch = list(exchange)
     for g in grads:
-        rows, width = g.shape[0] // groups, g.shape[1]
-        buffers += [
-            pltpu.VMEM((groups, rows // 2, width), BF),
-            pltpu.VMEM((groups, rows // 2, width), BF),
-            pltpu.VMEM((2, 2, rows // 4, width), BF),
-            pltpu.VMEM((2, rows // 4, width), BF),
-            pltpu.VMEM((2, rows // 4, width), BF),
-        ]
+        scratch += PlaneSum.scratch(g.shape, False)
+    for n in shards_out:
+        scratch += ColumnSum.scratch(*n)
     outs = pl.pallas_call(
-        partial(reduce_kernel, count, steps),
+        partial(reduce_kernel, (len(parts), batch, len(grads))),
         name="reduce_gradients",
-        in_specs=[smem, vmem] + [pl.BlockSpec(memory_space=pl.ANY)] * count,
-        out_specs=[vmem] + [vmem] * count,
-        out_shape=[jax.ShapeDtypeStruct(x.shape, x.dtype)]
-        + [jax.ShapeDtypeStruct((g.shape[0] // groups, g.shape[1]), BF) for g in grads],
-        scratch_shapes=[pltpu.VMEM(x.shape, x.dtype)] * 2
-        + [dma((2, size - 1)), dma((2, size - 1)), dma((2,)), dma((count, 2, 20))]
-        + buffers,
+        in_specs=[smem, vmem] + [vmem] * len(parts) + [pl.BlockSpec(memory_space=pl.ANY)] * len(grads),
+        out_specs=[vmem] * (1 + len(shards_out)),
+        out_shape=[jax.ShapeDtypeStruct(exchange[1].shape, x.dtype)]
+        + [jax.ShapeDtypeStruct(n, BF) for n in shards_out],
+        scratch_shapes=scratch,
         compiler_params=pltpu.CompilerParams(
             collective_id=1, has_side_effects=True, vmem_limit_bytes=67_043_328
         ),
-    )(table, x, *grads)
+    )(table, x, *parts, *grads)
     return outs[0], outs[1:]
 
 
@@ -876,6 +977,7 @@
         u2_ref[span, :] = u1 + bias_down[...] - jnp.mean(bias_down[...], axis=-1, keepdims=True)
 
     row_blocks(rows, 256, middle)
+    jobs.middle()
     waits[2]()
     waits[3]()
     block = 512
@@ -897,29 +999,13 @@
     sent()
 
 
-class NoJobs:
-    inputs = outputs = 0
-    arrays, shapes, scratch = (), (), ()
-
-    def __call__(self, guests, results, scratch):
-        return self
-
-    def start(self):
-        pass
-
-    def hook(self, number):
-        pass
-
-    def finish(self):
-        pass
-
-
 class GatherJobs:
     def __init__(self, layer, shards_in):
         groups = lax.axis_size("fsdp")
         self.layer = layer
         self.inputs = self.outputs = len(shards_in)
         self.arrays = tuple(shards_in)
+        self.in_specs = self.out_specs = [pl.BlockSpec(memory_space=pl.ANY)] * self.inputs
         self.shapes = tuple(
             jax.ShapeDtypeStruct((groups * s.shape[1], s.shape[2]), s.dtype) for s in shards_in
         )
@@ -946,7 +1032,7 @@
         for job in self.jobs:
             job.first()
 
-    def hook(self, number):
+    def middle(self):
         pass
 
     def finish(self):
@@ -954,6 +1040,38 @@
             job.second()
         for job in self.jobs:
             job.third()
+        for wait in self.pending:
+            wait()
+
+
+class RowJobs:
+    def __init__(self, to_runs_first, x, table, batch):
+        size, width = lax.axis_size("ctx"), x.shape[-1]
+        self.inputs, self.outputs = 2, 1
+        self.arrays = (table, x)
+        vmem = pl.BlockSpec(memory_space=pltpu.VMEM)
+        self.in_specs = [pl.BlockSpec(memory_space=pltpu.SMEM), vmem]
+        self.out_specs = [vmem]
+        self.scratch = tuple(Shuffle.scratch(to_runs_first, size, batch, x.size // width, width))
+        self.shapes = (jax.ShapeDtypeStruct(self.scratch[1].shape, x.dtype),)
+        self.kind = to_runs_first, batch
+
+    def __call__(self, guests, results, scratch):
+        self.pending = []
+        mid, turned, sems = scratch
+        self.job = Shuffle(
+            self.kind[0], guests[1], mid, turned, results[0], guests[0], sems, self.pending, self.kind[1]
+        )
+        return self
+
+    def start(self):
+        self.job.first()
+
+    def middle(self):
+        self.job.second()
+
+    def finish(self):
+        self.job.third()
         for wait in self.pending:
             wait()
 
@@ -968,8 +1086,8 @@
     outs = pl.pallas_call(
         partial(forward_kernel, runs, jobs),
         name=f"layer_forward_{number}",
-        in_specs=[vmem] * 6 + [hbm] * 4 + [hbm] * jobs.inputs,
-        out_specs=[vmem] * 8 + [hbm] + [hbm] * jobs.outputs,
+        in_specs=[vmem] * 6 + [hbm] * 4 + jobs.in_specs,
+        out_specs=[vmem] * 8 + [hbm] + jobs.out_specs,
         out_shape=[
             shape((rows, width), F32), shape((rows, width), BF), shape((rows, width), BF),
             shape((rows, 3 * width), BF), shape((rows, 2 * width), BF), shape((rows, width), BF),
@@ -1052,12 +1170,14 @@
     refs = refs[18:]
     gain1, gain2 = vec_ref.at[0:1, :], vec_ref.at[4:5, :]
     guests, refs = refs[: jobs_of.inputs], refs[jobs_of.inputs :]
-    g_ref, dvec, dbias_up, dw_qkv, dw_out, dw_up, dw_down = refs[:7]
+    g_ref, dvec, dbias_up, dw_qkv, dw_out, half_up, half_down = refs[:7]
     refs = refs[7:]
     dgain1, dbias_q, dbias_v, dbias_out, dgain2, dbias_down = (dvec.at[i : i + 1, :] for i in range(6))
     results, refs = refs[: jobs_of.outputs], refs[jobs_of.outputs :]
-    (vqkv, vout, vup, vdown, own_mask, past_mask, a2_ref, dy_ref, da_ref, dmix_ref, dqkv_ref, dpast_ref,
-     back_ref, come_ref, z_buf, sum0, sum1, sum2, sum3, load_sems, z_sems, out_sems, halo_sems) = refs[:23]
+    (vqkv, vout, vup, vdown, past_mask, a2_ref, dy_ref, da_ref, dmix_ref, dqkv_ref, dpast_ref,
+     come_ref, z_buf, load_sems, z_sems, out_sems, halo_sems) = refs[:17]
+    back_ref, own_mask = a2_ref, z_buf.at[1]
+    sums = [z_buf.at[0, :, n * 2 * HD : (n + 1) * 2 * HD] for n in range(4)]
     rows, width = u_ref.shape
     hidden = z_ref.shape[1]
     block = z_buf.shape[2]
@@ -1069,7 +1189,7 @@
 
     z_copy(0, 0).start()
     greet(lax.axis_size("ctx"), lax.axis_size("fsdp"))
-    jobs = jobs_of(guests, results, refs[23:])
+    jobs = jobs_of(guests, results, refs[17:], vdown, vup)
     jobs.start()
     for ref in (dvec, da_ref):
         ref[...] = jnp.zeros_like(ref)
@@ -1102,16 +1222,15 @@
         vdown[span, :] = dot_l(value.astype(BF), dy_ref[...]).astype(BF)
         da_ref[...] += dot_t(dz, vup[:, span])
         vup[:, span] = dot_l(a2_ref[...], dz).astype(BF)
+        jobs.tick("mlp", i)
         return 0
 
     lax.fori_loop(0, blocks, mlp, 0)
     stores = [
         pltpu.make_async_copy(src, dst, out_sems.at[n])
-        for n, (src, dst) in enumerate(((vdown, dw_down), (vup, dw_up), (vout, dw_out), (vqkv, dw_qkv)))
+        for n, (src, dst) in enumerate(((vout, dw_out), (vqkv, dw_qkv)))
     ]
-    stores[0].start()
-    stores[1].start()
-    jobs.hook(0)
+    jobs.tick("mid")
 
     def middle(span):
         du, part = norm_back_rows(da_ref[span, :], u1_ref[span, :], gain2[...])
@@ -1134,14 +1253,15 @@
         vout[span, :] = dot_l(mixed_ref[:, span], dy_ref[...]).astype(BF)
 
     column_blocks(0, width, 256, out_back)
-    stores[2].start()
+    stores[0].start()
     write_masks(own_mask, past_mask, sq[...], so[...], sp[...], True)
 
     def pair(i, _):
         attend_pair_back(
             pl.multiple_of(i * 2 * HD, 2 * HD), qkv_ref, past_ref, dmix_ref, mixed_ref, lse_ref,
-            own_mask, past_mask, dqkv_ref, dpast_ref, (sum0, sum1, sum2, sum3), width,
+            own_mask, past_mask, dqkv_ref, dpast_ref, sums, width,
         )
+        jobs.tick("pair", i)
         return 0
 
     lax.fori_loop(0, width // (2 * HD), pair, 0)
@@ -1151,7 +1271,7 @@
     sent, landed = send_rows(
         back_ref, come_ref, halo_sems, c - 1, jnp.logical_not(is_first), jnp.logical_not(is_last)
     )
-    jobs.hook(1)
+    jobs.tick("past")
     da_ref[...] = dot_t(dqkv_ref[...], vqkv[...])
 
     def qkv_back(span):
@@ -1171,7 +1291,8 @@
         return 0
 
     lax.fori_loop(0, 2 * width // 256, kv_back, 0)
-    stores[3].start()
+    stores[1].start()
+    jobs.tick("qkv")
     landed()
 
     @pl.when(is_last)
@@ -1185,10 +1306,123 @@
         g_ref[span, :] = g_ref[span, :] + du
 
     row_blocks(rows, 128, tail)
-    jobs.finish()
+    jobs.finish(half_down, half_up, out_sems)
     for store in stores:
         store.wait()
     sent()
+
+
+class BackJobs:
+    def __init__(self, shapes, parts, grads, rows):
+        groups = lax.axis_size("fsdp")
+        vmem, hbm = pl.BlockSpec(memory_space=pltpu.VMEM), pl.BlockSpec(memory_space=pl.ANY)
+        self.parts, self.planes, self.rows = len(parts), len(grads), rows
+        self.arrays = (*parts, *grads, *(rows.arrays if rows else ()))
+        self.in_specs = [vmem] * self.parts + [hbm] * self.planes + (rows.in_specs if rows else [])
+        totals = [(2 * p.shape[0], p.shape[1]) for p in parts]
+        totals += [(g.shape[0] // groups, g.shape[1]) for g in grads]
+        self.shapes = tuple(jax.ShapeDtypeStruct(n, BF) for n in totals)
+        self.out_specs = [vmem] * len(totals)
+        self.scratch = ()
+        if rows:
+            self.shapes += rows.shapes
+            self.out_specs = self.out_specs + rows.out_specs
+            self.scratch += rows.scratch
+        self.inputs, self.outputs = len(self.arrays), len(self.shapes)
+        for shape in shapes:
+            self.scratch += PlaneSum.scratch(shape, True)
+        for g in grads:
+            self.scratch += PlaneSum.scratch(g.shape, False)
+        for n in totals:
+            self.scratch += ColumnSum.scratch(*n)
+
+    def __call__(self, guests, results, scratch, vdown, vup):
+        guests, results, refs = Refs(guests), Refs(results), Refs(scratch)
+        parts, grads = guests.take(self.parts), guests.take(self.planes)
+        totals = results.take(self.parts + self.planes)
+        self.pending = []
+        plan = {}
+
+        def put(point, *work):
+            plan.setdefault(point, []).extend(work)
+
+        if self.rows:
+            job = self.rows(guests.take(2), results.take(1), refs.take(3)).job
+            job.pending = self.pending
+            put(("start", 0), job.first)
+            put(("mlp", 3), job.second)
+            put(("end", 0), job.third)
+        self.own = []
+        for v in (vdown, vup):
+            pair, half, quarter, sems = refs.take(4)
+            self.own.append(PlaneSum(v, pair, half, quarter, None, sems, self.pending))
+        planes = []
+        for g in grads:
+            pair, half, quarter, stage, sems = refs.take(5)
+            planes.append(PlaneSum(g, pair, half, quarter, stage, sems, self.pending))
+        columns = []
+        for i, total in enumerate(totals):
+            column, sems = refs.take(2)
+            if i < self.parts:
+                s = parts[i].shape[0] // 2
+                part = lambda q, i=i, s=s: parts[i].at[pl.ds(q * s, s), :]
+            else:
+                part = lambda q, job=planes[i - self.parts]: job.colour(job.f, q)
+            columns.append(ColumnSum(part, column, total, sems, self.pending))
+        for job in planes:
+            put(("start", 0), job.step0)
+        early = [("start", 0), ("mlp", 0), ("mlp", 1), ("mlp", 2), ("mlp", 3), ("mlp", 4), ("mlp", 5)]
+        for c in columns[: self.parts]:
+            for point, hop in zip(early, c.hops()):
+                put(point, hop)
+        for job in planes:
+            put(("mlp", 1), job.step1)
+            put(("mlp", 3), job.step2)
+            put(("mlp", 5), job.step3)
+        for job in self.own:
+            put(("mid", 0), job.step0)
+        late = [("mid", 0), ("pair", 0), ("pair", 1), ("pair", 2), ("pair", 3), ("pair", 4), ("pair", 5)]
+        for c in columns[self.parts :]:
+            for point, hop in zip(late, c.hops()):
+                put(point, hop)
+        down, up = self.own
+        put(("pair", 0), down.step1)
+        put(("pair", 1), up.step1)
+        put(("pair", 4), down.step2)
+        put(("past", 0), up.step2)
+        put(("qkv", 0), down.step3)
+        put(("end", 0), up.step3)
+        for c in columns:
+            put(("end", 0), c.finish)
+        self.plan = plan
+        return self
+
+    def run(self, point):
+        for work in self.plan.get(point, ()):
+            work()
+
+    def start(self):
+        self.run(("start", 0))
+
+    def tick(self, name, index=None):
+        if index is None:
+            self.run((name, 0))
+            return
+        for k in range(8):
+            if (name, k) in self.plan:
+                pl.when(index == k)(partial(self.run, (name, k)))
+
+    def finish(self, half_down, half_up, sems):
+        self.run(("end", 0))
+        copies = []
+        for n, (job, out) in enumerate(zip(self.own, (half_down, half_up))):
+            copy = pltpu.make_async_copy(job.acc(job.f), out, sems.at[2 + n])
+            copy.start()
+            copies.append(copy)
+        for wait in self.pending:
+            wait()
+        for copy in copies:
+            copy.wait()
 
 
 def fused_backward(g, u, saved, vec, matrices, segs, runs, jobs, number):
@@ -1203,20 +1437,20 @@
     outs = pl.pallas_call(
         partial(backward_kernel, runs, jobs),
         name=f"layer_backward_{number}",
-        in_specs=[vmem] * 13 + [hbm] * 5 + [vmem] * jobs.inputs,
-        out_specs=[vmem] * 3 + [hbm] * 4 + [vmem] * jobs.outputs,
+        in_specs=[vmem] * 13 + [hbm] * 5 + jobs.in_specs,
+        out_specs=[vmem] * 3 + [hbm] * 4 + jobs.out_specs,
         out_shape=[
             shape((rows, width), F32), shape((6, width), F32), shape((1, hidden), F32),
-            *(shape(x.shape, BF) for x in (w_qkv, w_out, w_up, w_down)), *jobs.shapes,
+            *(shape(x.shape, BF) for x in (w_qkv, w_out)),
+            *(shape((x.shape[0] // 8, x.shape[1]), BF) for x in (w_up, w_down)), *jobs.shapes,
         ],
         scratch_shapes=[
             *(pltpu.VMEM(x.shape, BF) for x in (w_qkv, w_out, w_up, w_down)),
-            pltpu.VMEM((rows, rows), F32), pltpu.VMEM((rows, rows), F32),
+            pltpu.VMEM((rows, rows), F32),
             pltpu.VMEM((rows, width), BF), pltpu.VMEM((rows, width), BF), pltpu.VMEM((rows, width), F32),
             pltpu.VMEM((rows, width), BF), pltpu.VMEM((rows, 3 * width), BF),
-            pltpu.VMEM((rows, 2 * width), BF), pltpu.VMEM((rows, width), BF), pltpu.VMEM((rows, width), BF),
+            pltpu.VMEM((rows, 2 * width), BF), pltpu.VMEM((rows, width), BF),
             pltpu.VMEM((2, rows, 512), F32),
-            *(pltpu.VMEM((rows, 2 * HD), F32) for _ in range(4)),
             dma((4,)), dma((2,)), dma((4,)), dma((2,)), *jobs.scratch,
         ],
         compiler_params=pltpu.CompilerParams(
@@ -1226,7 +1460,7 @@
         g, u, a1, a1p, qkv, past, mixed, lse, u1, vec,
         seg_row, seg_col, seg_past.reshape(-1, 1), z, w_qkv, w_out, w_up, w_down, *jobs.arrays,
     )
-    return outs[0], outs[1], outs[2], dict(zip(MATRICES, outs[3:7])), outs[7:]
+    return outs[0], outs[1], outs[2], outs[3:7], outs[7:]
 
 
 VECTORS = (0, 2, 3, 5, 6, 10)
@@ -1250,22 +1484,15 @@
 
     blocks = jnp.arange(2 * size, dtype=jnp.int32)
     place = jnp.sum(jnp.where(block_order[None, :] == blocks[:, None], blocks[None, :], 0), axis=1)
-    table = jnp.stack(
-        [
-            jnp.concatenate([place // 2] * batch),
-            jnp.concatenate([b * 2 + place % 2 for b in range(batch)]),
-        ]
-    )
+    near = size // batch
+    to_table = jnp.stack([place // 2, place % 2])
+    from_table = jnp.stack([block_order // (2 * batch), block_order % (2 * batch)])
     pad = [(0, 0), (0, 0), (0, 1)]
-    both = jnp.concatenate([jnp.pad(block_input[:, 0], pad), jnp.pad(cotangent[:, 0], pad)], axis=2)
-    x = both.reshape(batch, 2, size, block // size, 2 * width).transpose(2, 0, 1, 3, 4)
-    x = x.reshape(size, 2 * batch, block // size, 2 * width)
+    x, ct = (for_runs(jnp.pad(v[:, 0], pad), size) for v in (block_input, cotangent))
     short = jnp.stack([weights[m] for m in VECTORS], axis=1)
     packed = jnp.concatenate([short.reshape(-1), weights[LONG].reshape(-1)])
     packed = pad_to(packed, lines * 128).reshape(lines, 128)
-    x, packed, full = gather_all(
-        x, table, run_steps(size, batch), 0, packed, [weights[m] for m in MATRICES]
-    )
+    x, packed, full = gather_all(x, to_table, 0, batch, packed, [weights[m] for m in MATRICES])
     packed = packed.reshape(groups, lines * 128)
     cut = layers * many * width // groups
     short = packed[:, :cut].reshape(groups, layers * many, width // groups)
@@ -1273,44 +1500,45 @@
     long = packed[:, cut:each].reshape(groups, layers, hidden // groups)
     long = long.transpose(1, 0, 2).reshape(layers, 1, hidden).astype(F32)
 
-    both = x.transpose(1, 0, 2, 3).reshape(run, 2 * width).astype(F32)
-    h, g = both[:, :width], both[:, width:]
+    h = of_runs(x).astype(F32)
     u = h - jnp.pad(jnp.sum(h, axis=1, keepdims=True), [(0, 0), (width - 1, 0)])
     kept, matrices = [], [full]
     for layer in range(layers):
-        more = layer + 1 < layers
-        jobs = GatherJobs(layer + 1, [weights[m] for m in MATRICES]) if more else NoJobs()
+        if layer + 1 < layers:
+            jobs = GatherJobs(layer + 1, [weights[m] for m in MATRICES])
+        else:
+            jobs = RowJobs(True, ct, to_table, batch)
         u_in = u
         u, saved, full = fused_forward(u, short[layer], long[layer], matrices[layer], segs, runs, jobs, layer)
         kept.append((u_in, saved))
         matrices.append(full)
-    dshort, dlong, grads = [None] * layers, [None] * layers, [None] * layers
+    g = of_runs(full[0]).astype(F32)
+    out = RowJobs(False, for_store(u.astype(BF), near, 2 * batch), from_table, batch)
+    shapes = [matrices[0][3].shape, matrices[0][2].shape]
+    dshort, dlong, found = [None] * layers, [None] * layers, {}
+    parts, grads = [], []
     for layer in reversed(range(layers)):
-        g, dshort[layer], dlong[layer], grads[layer], _ = fused_backward(
-            g, *kept[layer], short[layer], matrices[layer], segs, runs, NoJobs(), layer
+        last = layer == layers - 1
+        jobs = BackJobs(shapes, parts, grads, out if last else None)
+        g, dshort[layer], dlong[layer], (dw_qkv, dw_out, half_up, half_down), done = fused_backward(
+            g, *kept[layer], short[layer], matrices[layer], segs, runs, jobs, layer
         )
-    both = jnp.concatenate([u.astype(BF), (g - g[:, narrow:]).astype(BF)], axis=1)
-    table = jnp.stack(
-        [
-            jnp.concatenate([b * runs + block_order // (2 * batch) for b in range(batch)]),
-            jnp.concatenate([block_order % (2 * batch)] * batch),
-        ]
-    ).astype(jnp.int32)
-    x = both.reshape(2 * batch, size, block // size, 2 * width).transpose(1, 0, 2, 3)
+        if last:
+            out = of_store(done[-1], batch)
+        else:
+            found.update(zip([(layer + 1, m) for m in (9, 7, 4, 1)], done))
+        parts, grads = [half_down, half_up], [dw_out, dw_qkv]
     short = jnp.concatenate(dshort).reshape(layers * many, groups, width // groups)
     long = jnp.concatenate(dlong).reshape(layers, groups, hidden // groups)
     packed = jnp.concatenate(
         [v.transpose(1, 0, 2).reshape(groups, -1).astype(BF) for v in (short, long)], axis=1
     )
     packed = pad_to(packed, grad_lines * 128).reshape(groups * grad_lines, 128)
-    order = [(layer, m) for layer in reversed(range(layers)) for m in (9, 7, 4, 1)]
-    x, sums = reduce_all(
-        x, table, store_steps(size, batch), [grads[layer][m] for layer, m in order] + [packed]
-    )
-    both = x.reshape(size, batch, 2, block // size, 2 * width).transpose(1, 2, 0, 3, 4)
-    both = both.reshape(batch, rows, 2 * width)
+    x = for_store((g - g[:, narrow:]).astype(BF), near, 2 * batch)
+    x, sums = reduce_all(x, from_table, batch, parts, grads + [packed])
+    found.update(zip([(0, m) for m in (9, 7, 4, 1)], sums))
+    d_in = of_store(x, batch)
     totals = [None] * 11
-    found = dict(zip(order, sums))
     for m in MATRICES:
         totals[m] = jnp.stack([found[layer, m] for layer in range(layers)]).astype(F32)
     flat = sums[-1].reshape(-1).astype(F32)
@@ -1318,9 +1546,7 @@
     for n, m in enumerate(VECTORS):
         totals[m] = short[:, n]
     totals[LONG] = flat[cut:each].reshape(layers, hidden // groups)
-    out = both[:, None, :, :narrow]
-    d_in = both[:, None, :, width : width + narrow].astype(F32)
-    return (out, d_in, *totals)
+    return (out[:, None, :, :narrow], d_in[:, None, :, :narrow].astype(F32), *totals)
 
 
 def step_plain(block_input, cotangent, block_order, weights, segs, size, shift):

time: 553 us -> 534 us (0.966)
  Pallas kernels: 498 us -> 479 us
  other arithmetic: 21.7 us -> 15.8 us
  local copies, waits for them, and re-layouts: 27.5 us -> 33.1 us
    pallas_call x2, Pallas kernels: 261 us -> 170 us  [the longest x1 99.8 us: reduce_all(): pl.pallas_call(partial(reduce_kernel, (len(parts), batch, len(grads))), n...]
    pallas_call x2, Pallas kernels: 121 us -> 190 us  [fused_backward(): pl.pallas_call(partial(backward_kernel, runs, jobs), name=f'layer_backwar...]
    unnamed x58 -> x53, local copies, waits for them, and re-layouts: 14.9 us -> 16.9 us
where the time goes in v1:
time: 534 us; the launch traced here: 529 us
  Pallas kernels  479 us (90%)
  local copies, waits for them, and re-layouts  33.1 us (6%)
  other arithmetic  15.8 us (3%)
    pallas_call x2, Pallas kernels, fused_backward(): pl.pallas_call(partial(backward_kernel, runs, jobs), name=f'layer_backwar...  190 us
    pallas_call x2, Pallas kernels, fused_forward(): pl.pallas_call(partial(forward_kernel, runs, jobs), name=f'layer_forward_...  119 us
    pallas_call x1, Pallas kernels, reduce_all(): pl.pallas_call(partial(reduce_kernel, (len(parts), batch, len(grads))), n...  99.8 us
    pallas_call x1, Pallas kernels, gather_all(): pl.pallas_call(partial(gather_kernel, layer, count, batch), name='gather_...  70.3 us
    unnamed x53, local copies, waits for them, and re-layouts  16.9 us

profile of v1, /device:TPU:0, one launch (start us, length us, event | category | flops | bytes accessed | tf_op | source)
XLA Modules:
  0.0 529.4 jit_solution(9429686039255891378)
XLA Ops:
  0.7 0.8 select_reduce_fusion
  2.0 0.7 fusion.9
  3.3 0.7 reshape.212
  4.0 0.7 constant_dynamic-update-slice_fusion.5
  4.7 0.7 constant_dynamic-update-slice_fusion.4
  5.3 0.7 constant_dynamic-update-slice_fusion.3
  6.0 0.7 constant_dynamic-update-slice_fusion.2
  6.7 0.7 constant_dynamic-update-slice_fusion.1
  7.4 0.7 constant_dynamic-update-slice_fusion
  8.2 0.6 fusion.7.refs_2_
  8.8 0.7 constant_dynamic-slice_fusion
  9.6 0.9 copy.98.refs_3_.refs_11_
  10.5 0.9 copy.106.refs_12_
  11.3 2.2 copy.90
  13.6 0.9 copy.91
  14.9 1.2 copy.100
  16.1 0.9 copy.101
  17.1 70.3 %gather_weights.1 = (bf16[4,4,32,768]{3,2,1,0:T(8,128)(2,1)}, bf16[128,128]{1,0:T(8,128)(2,1)}, bf16[768,2304]{1,0:T(8,128)(2,1)}, bf16[768,768]{1,0:T(8,128)(2,...) custom-call(s32[2,16]{1,0:T(2,128)} %pad_add_fusion.refs_0_.refs_10_, bf16[8,2,32,768]{3,2,1,0:T(8,128)(2,1)} %bitcast.117, ...), custom_call_target="tpu_custom_call" | custom-call | tf_op jit(solution)/shard_map/gather_weights/pallas_call | solution.py:515
  87.3 0.8 reshape.214
  88.2 1.3 convert_reduce_fusion
  89.6 0.6 copy.122
  90.2 0.6 copy.121
  90.9 0.7 squeeze.47.refs_1_.refs_9_
  91.6 0.7 squeeze.44.refs_1_.refs_9_
  92.8 1.3 bitcast_subtract_fusion.refs_0_.refs_1_
  94.1 73.4 %layer_forward_0.1 = (f32[512,768]{1,0:T(8,128)}, bf16[512,768]{1,0:T(8,128)(2,1)}, bf16[512,768]{1,0:T(8,128)(2,1)}, bf16[512,2304]{1,0:T(8,128)(2,1)}, bf16[51...) custom-call(f32[512,768]{1,0:T(8,128)} %bitcast_subtract_fusion.refs, ...), custom_call_target="tpu_custom_call" | custom-call | tf_op jit(solution)/shard_map/layer_forward_0/pallas_call | solution.py:1086
  167.5 45.5 %layer_forward_1.1 = (f32[512,768]{1,0:T(8,128)}, bf16[512,768]{1,0:T(8,128)(2,1)}, bf16[512,768]{1,0:T(8,128)(2,1)}, bf16[512,2304]{1,0:T(8,128)(2,1)}, bf16[51...) custom-call(f32[512,768]{1,0:T(8,128)} %get-tuple-element.73.refs_0_, ...), custom_call_target="tpu_custom_call" | custom-call | tf_op jit(solution)/shard_map/layer_forward_1/pallas_call | solution.py:1086
  213.0 1.3 convert_bitcast_fusion.1
  214.3 1.3 copy.103
  215.6 0.7 copy-done.2
  216.4 0.9 copy.133
  217.3 77.8 %layer_backward_1.1 = (f32[512,768]{1,0:T(8,128)}, f32[6,768]{1,0:T(8,128)}, f32[1,3072]{1,0:T(1,128)}, bf16[768,2304]{1,0:T(8,128)(2,1)}, bf16[768,768]{1,0:T(8...) custom-call(f32[512,768]{1,0:T(8,128)} %bitcast.116, ...), custom_call_target="tpu_custom_call" | custom-call | tf_op jit(solution)/shard_map/layer_backward_1/pallas_call | solution.py:1437
  295.1 112.4 %layer_backward_0.1 = (f32[512,768]{1,0:T(8,128)}, f32[6,768]{1,0:T(8,128)}, f32[1,3072]{1,0:T(1,128)}, bf16[768,2304]{1,0:T(8,128)(2,1)}, bf16[768,768]{1,0:T(8...) custom-call(f32[512,768]{1,0:T(8,128)} %get-tuple-element.89.refs_0_, ...), custom_call_target="tpu_custom_call" | custom-call | tf_op jit(solution)/shard_map/layer_backward_0/pallas_call | solution.py:1437
  407.5 1.2 copy.107
  408.8 1.8 copy.113
  411.0 0.9 copy.132
  412.4 0.7 reshape.222.refs_6_
  413.1 99.8 %reduce_gradients.1 = (bf16[8,2,32,768]{3,2,1,0:T(8,128)(2,1)}, bf16[768,768]{1,0:T(8,128)(2,1)}, bf16[192,3072]{1,0:T(8,128)(2,1)}, bf16[192,768]{1,0:T(8,128)(...) custom-call(s32[2,16]{1,0:T(2,128)} %pad_add_fusion.1.refs_18_.refs_0_, bf16[4,4,32,768]{3,2,1,0:T(8,128)(2,1)} %bitcast.126, ...), custom_call_target="tpu_custom_call" | custom-call | tf_op jit(solution)/shard_map/reduce_gradients/pallas_call | solution.py:792
  512.9 1.2 copy.112
  514.2 0.6 reshape.226
  514.8 0.6 copy_bitcast_fusion.3
  515.4 0.6 copy_bitcast_fusion.5
  516.7 2.8 copy.114
  519.5 1.1 maximum_convert_fusion.3
  521.4 2.0 maximum_convert_fusion.2
  523.4 0.7 copy-done.6
  524.1 2.5 maximum_convert_fusion
  526.7 2.5 maximum_convert_fusion.1
  (78 shorter events, 4.9 us)
Async XLA Ops:
  9.6 0.9 copy-start.12
  9.6 0.9 copy-start.13
  13.6 1.3 copy-start.9
  87.3 5.2 copy-start
  214.3 2.0 copy-start.2
  408.7 1.9 copy-start.1
  410.8 1.1 copy-start.16
  410.8 1.1 copy-start.18
  410.8 1.1 copy-start.15
  410.8 1.4 copy-start.17
  512.9 1.2 copy-start.14
  516.7 2.8 copy-start.10
  516.7 2.8 copy-start.11
  519.5 1.6 copy-start.7
  519.5 1.9 copy-start.8
  521.4 2.0 copy-start.4
  521.4 2.8 copy-start.6
  524.1 2.5 copy-start.3
  524.1 2.6 copy-start.5
